TPU v7x, 32 devices: a whole 2x2x4 slice. The times are simulated.
32 devices in a mesh: dp: 4 (over y, x), seq: 8 (over z, core).
Axes of the slice: x: 2, y: 2, z: 4, core: 2. Of those that a mesh axis runs over, the one named last changes fastest.
Arguments:
- tokens: float32 [4, 1024, 1024], P('dp', 'seq'), may hold values from -6 to 6
- cotangent: float32 [4, 1024, 1024], P('dp', 'seq'), may hold values from -6 to 6
- doc_ids: int32 [4, 1024], P('dp'), may hold values from 0 to 1, never falling along the last dimension, each value on 1 to 768 neighbouring positions
- in_weight: float32 [1024, 4384], P(('dp', 'seq')), may hold values from -0.1875 to 0.1875
- out_weight: float32 [1024, 2048], P(('dp', 'seq')), may hold values from -0.125 to 0.125
- in_m: float32 [1024, 4384], P(('dp', 'seq')), may hold values from -30 to 30
- in_v: float32 [1024, 4384], P(('dp', 'seq')), may hold values from 1 to 1000
- out_m: float32 [1024, 2048], P(('dp', 'seq')), may hold values from -30 to 30
- out_v: float32 [1024, 2048], P(('dp', 'seq')), may hold values from 1 to 1000
- vec_params: float32 [14688], replicated, as said below
- vec_m: float32 [14688], replicated, may hold values from -30 to 30
- vec_v: float32 [14688], replicated, may hold values from 1 to 1000
Outputs:
- activations: float32 [4, 1024, 1024], P('dp', 'seq')
- input_grad: float32 [4, 1024, 1024], P('dp', 'seq')
- in_grad: float32 [1024, 4384], P(('dp', 'seq'))
- out_grad: float32 [1024, 2048], P(('dp', 'seq'))
- vec_grad: float32 [14688], replicated
- in_new: float32 [1024, 4384], P(('dp', 'seq'))
- out_new: float32 [1024, 2048], P(('dp', 'seq'))
- vec_new: float32 [14688], replicated
- in_m_new: float32 [1024, 4384], P(('dp', 'seq'))
- in_v_new: float32 [1024, 4384], P(('dp', 'seq'))
- out_m_new: float32 [1024, 2048], P(('dp', 'seq'))
- out_v_new: float32 [1024, 2048], P(('dp', 'seq'))
- vec_m_new: float32 [14688], replicated
- vec_v_new: float32 [14688], replicated
Inputs may be any that keep to these rules, and one draw needn't show every extreme that they name: `doc_ids`: each row holds document 0 and then document 1, each of one or more positions, none longer than 768. `vec_params`: norm_gain and gate_gain lie in 0.7 to 1.3, skip_gain in 0.5 to 1.5, step_bias in -1 to 1, log_rate in -12 to -3.
All inputs are finite; a program needn't handle non-finite values.
Results may differ from a plain program's by a relative error of at most 0.015.
Values may be sent and summed in bfloat16 or wider, within the bound.
A program may use at most 192 MiB of HBM per device.

v0:
```python
import jax
import jax.numpy as jnp
from jax import lax
from jax.sharding import PartitionSpec as P

D = 1024
DI = 2048
H = 32
P_SIZE = 64
N = 128
KW = 4
STRETCH = 256
STEP = 10
CONV = 2304


norm_eps = 1e-05
beta_one = 0.9
beta_two = 0.95
learn_rate = 0.03
decay_rate = 0.1
adam_eps = 1e-08
top_precision = lax.Precision.HIGHEST


def shifted_2(block, axis, distance):
    devices = range(lax.axis_size(axis))
    route = [(i - distance, i) for i in devices if i - distance in devices]
    return lax.ppermute(block, axis, route)


def unpack(vector):
    cursor = D + DI
    norm_gain = vector[:D]
    gate_gain = vector[D:cursor]
    conv_kernel = vector[cursor : cursor + KW * CONV].reshape(KW, CONV)
    cursor = cursor + KW * CONV
    conv_bias = vector[cursor : cursor + CONV]
    cursor = cursor + CONV
    step_bias = vector[cursor : cursor + H]
    log_rate = vector[cursor + H : cursor + 2 * H]
    skip_gain = vector[cursor + 2 * H : cursor + 3 * H]
    return (norm_gain, gate_gain, conv_kernel, conv_bias, step_bias, log_rate, skip_gain)


def repack(norm_gain, gate_gain, conv_kernel, conv_bias, step_bias, log_rate, skip_gain):
    return jnp.concatenate(
        [norm_gain, gate_gain, conv_kernel.reshape(-1), conv_bias, step_bias, log_rate, skip_gain]
    )


def input_norm(inputs, gain):
    scale = lax.rsqrt(jnp.mean(inputs * inputs, axis=-1, keepdims=True) + norm_eps)
    return inputs * scale * gain[None, :]


def gate_norm(ssd_out, gate_in, gain):
    mixed = ssd_out * jax.nn.silu(gate_in)
    scale = lax.rsqrt(jnp.mean(mixed * mixed, axis=-1, keepdims=True) + norm_eps)
    return mixed * scale * gain[None, :]


def conv_silu(padded, conv_kernel, conv_bias, ext_ids):
    length = padded.shape[0] - (KW - 1)
    own_ids = ext_ids[KW - 1 :]
    total = jnp.zeros((length, padded.shape[1]), jnp.float32) + conv_bias[None, :]
    for offset in range(KW):
        valid = (ext_ids[offset : offset + length] == own_ids).astype(jnp.float32)
        total = (
            total + conv_kernel[offset][None, :] * padded[offset : offset + length] * valid[:, None]
        )
    return jax.nn.silu(total)


def rates(step_raw, step_bias, log_rate):
    step_size = jax.nn.softplus(step_raw + step_bias[None, :])
    log_decay = -jnp.exp(log_rate)[None, :] * step_size
    return (step_size, log_decay)


def ssd_block(state, pieces):
    values, input_map, output_map, step_size, log_decay, block_ids, prior_id = pieces
    length = values.shape[0]
    cumulative = jnp.cumsum(log_decay, axis=0)
    rows_index = lax.broadcasted_iota(jnp.int32, (length, length), 0)
    cols_index = lax.broadcasted_iota(jnp.int32, (length, length), 1)
    related = (block_ids[:, None] == block_ids[None, :]) & (rows_index >= cols_index)
    spans = cumulative.T[:, :, None] - cumulative.T[:, None, :]
    decays = jnp.where(related[None], jnp.exp(jnp.where(related[None], spans, 0.0)), 0.0)
    scores = jnp.dot(output_map, input_map.T, precision=top_precision)
    mixing = decays * scores[None] * step_size.T[:, None, :]
    inside = jnp.einsum("hij,jhp->ihp", mixing, values, precision=top_precision)
    carried = (block_ids == prior_id).astype(jnp.float32)
    reach = carried[:, None] * jnp.exp(cumulative)
    entering = (
        jnp.einsum("hpn,in->ihp", state, output_map, precision=top_precision) * reach[:, :, None]
    )
    ending = (block_ids == block_ids[-1]).astype(jnp.float32)
    tail_weight = ending[:, None] * jnp.exp(cumulative[-1][None, :] - cumulative) * step_size
    new_state = state * reach[-1][:, None, None] + jnp.einsum(
        "jh,jhp,jn->hpn", tail_weight, values, input_map, precision=top_precision
    )
    return (new_state, inside + entering)


def ssd_run(mixed_in, step_size, log_decay, skip_gain, row_ids, prior_id, state, block):
    length = mixed_in.shape[0]
    blocks = length // block
    values = mixed_in[:, :DI].reshape(length, H, P_SIZE)
    input_map = mixed_in[:, DI : DI + N]
    output_map = mixed_in[:, DI + N :]
    shifted = jnp.concatenate([jnp.reshape(prior_id, (1,)), row_ids[:-1]])
    priors = shifted.reshape(blocks, block)[:, 0]
    pieces = (
        values.reshape(blocks, block, H, P_SIZE),
        input_map.reshape(blocks, block, N),
        output_map.reshape(blocks, block, N),
        step_size.reshape(blocks, block, H),
        log_decay.reshape(blocks, block, H),
        row_ids.reshape(blocks, block),
        priors,
    )
    final, outputs = lax.scan(ssd_block, state, pieces)
    result = outputs.reshape(length, H, P_SIZE) + skip_gain[None, :, None] * values
    return (result.reshape(length, DI), final)


def adamw_update(param, grad, first, second):
    first_new = beta_one * first + (1.0 - beta_one) * grad
    second_new = beta_two * second + (1.0 - beta_two) * grad * grad
    corrected = first_new / (1.0 - beta_one**STEP)
    scaled = jnp.sqrt(second_new / (1.0 - beta_two**STEP)) + adam_eps
    return (
        param * (1.0 - learn_rate * decay_rate) - learn_rate * corrected / scaled,
        first_new,
        second_new,
    )


def body(
    tokens,
    cotangent,
    doc_ids,
    in_weight,
    out_weight,
    in_m,
    in_v,
    out_m,
    out_v,
    vec_params,
    vec_m,
    vec_v,
):
    in_work, out_work = (
        lax.all_gather(in_weight.astype(jnp.bfloat16), ("dp", "seq"), axis=0, tiled=True),
        lax.all_gather(out_weight.astype(jnp.bfloat16), ("dp", "seq"), axis=0, tiled=True),
    )
    norm_gain, gate_gain, conv_kernel, conv_bias, step_bias, log_rate, skip_gain = unpack(
        vec_params
    )
    inputs = tokens[0]
    upstream_f = cotangent[0]
    local_len = inputs.shape[0]
    block = min(STRETCH, local_len)
    padded_row = jnp.concatenate([jnp.full((KW - 1,), -1, jnp.int32), doc_ids[0]])
    offset = lax.axis_index("seq") * local_len
    ext_ids = lax.dynamic_slice_in_dim(padded_row, offset, local_len + KW - 1)
    own_ids = ext_ids[KW - 1 :]
    prior_id = ext_ids[KW - 2]
    zero_state = jnp.zeros((H, P_SIZE, N), jnp.float32)
    normed = input_norm(inputs, norm_gain).astype(jnp.bfloat16)
    projected = jnp.dot(normed, in_work, preferred_element_type=jnp.float32)
    gate_in = projected[:, :DI]
    conv_in = projected[:, DI : DI + CONV].astype(jnp.bfloat16)
    step_raw = projected[:, DI + CONV :]
    rim = shifted_2(conv_in[local_len - (KW - 1) :], "seq", 1)
    padded = lax.optimization_barrier(jnp.concatenate([rim, conv_in], axis=0)).astype(jnp.float32)
    mixed_in = lax.optimization_barrier(
        conv_silu(padded, conv_kernel, conv_bias, ext_ids).astype(jnp.bfloat16)
    ).astype(jnp.float32)
    output_map = mixed_in[:, DI + N :]

    def pre_chain(mixed, raw, bias_in, rate_in, skip_in):
        step_size, log_decay = rates(raw, bias_in, rate_in)
        local_out, local_state = ssd_run(
            mixed, step_size, log_decay, skip_in, own_ids, prior_id, zero_state, block
        )
        cumulative = jnp.cumsum(log_decay, axis=0)
        reach = (own_ids == prior_id).astype(jnp.float32)[:, None] * jnp.exp(cumulative)
        return (local_out, local_state, reach)

    local_out, local_state, reach = pre_chain(mixed_in, step_raw, step_bias, log_rate, skip_gain)
    decay = reach[-1]

    def relay(turn, entry_now):
        return shifted_2(decay[:, None, None] * entry_now + local_state, "seq", 1)

    entry = lax.fori_loop(0, lax.axis_size("seq") - 1, relay, zero_state)
    entering = (
        jnp.einsum("hpn,tn->thp", entry, output_map, precision=top_precision) * reach[:, :, None]
    )
    ssd_out = local_out + entering.reshape(local_len, DI)
    gated, gate_back = jax.vjp(gate_norm, ssd_out, gate_in, gate_gain)
    normed_out = gated.astype(jnp.bfloat16)
    outputs = inputs + lax.dot_general(
        normed_out, out_work, (((1,), (1,)), ((), ())), preferred_element_type=jnp.float32
    )
    upstream = upstream_f.astype(jnp.bfloat16)
    grad_gated = jnp.dot(upstream, out_work, preferred_element_type=jnp.float32)
    grad_ssd, grad_gate_in, grad_gate_gain = gate_back(grad_gated)
    own_part = jnp.einsum(
        "th,thp,tn->hpn",
        reach,
        grad_ssd.reshape(local_len, H, P_SIZE),
        output_map,
        precision=top_precision,
    )

    def back_relay(turn, later):
        return shifted_2(
            (own_part + decay[:, None, None] * later).astype(jnp.bfloat16), "seq", -1
        ).astype(jnp.float32)

    after = lax.fori_loop(0, lax.axis_size("seq") - 1, back_relay, zero_state)

    def complete(mixed, raw, bias_in, rate_in, skip_in):
        part_out, part_state, part_reach = pre_chain(mixed, raw, bias_in, rate_in, skip_in)
        reader = mixed[:, DI + N :]
        arriving = (
            jnp.einsum("hpn,tn->thp", entry, reader, precision=top_precision)
            * part_reach[:, :, None]
        )
        return (part_out + arriving.reshape(local_len, DI), part_reach[-1], part_state)

    _, ssd_back = jax.vjp(complete, mixed_in, step_raw, step_bias, log_rate, skip_gain)
    grad_mixed, grad_raw, grad_bias, grad_rate, grad_skip = ssd_back(
        (grad_ssd, jnp.sum(after * entry, axis=(1, 2)), after)
    )
    _, conv_back = jax.vjp(
        lambda values, kernel, constant: conv_silu(values, kernel, constant, ext_ids),
        padded,
        conv_kernel,
        conv_bias,
    )
    grad_padded, grad_kernel, grad_cbias = conv_back(grad_mixed)
    returned = shifted_2(grad_padded[: KW - 1], "seq", -1)
    grad_conv = jnp.concatenate(
        [grad_padded[KW - 1 : local_len], grad_padded[local_len:] + returned], axis=0
    )
    grad_proj = jnp.concatenate([grad_gate_in, grad_conv, grad_raw], axis=1).astype(jnp.bfloat16)
    grad_normed = lax.dot_general(
        grad_proj, in_work, (((1,), (1,)), ((), ())), preferred_element_type=jnp.float32
    )
    _, norm_back = jax.vjp(input_norm, inputs, norm_gain)
    grad_inputs, grad_norm_gain = norm_back(grad_normed)
    vector = repack(
        grad_norm_gain, grad_gate_gain, grad_kernel, grad_cbias, grad_bias, grad_rate, grad_skip
    )
    dp_count = lax.axis_size("dp")
    seq_count = lax.axis_size("seq")
    owner_rows = in_weight.shape[0]
    seq_place = lax.axis_index("seq")

    def select_rows(matrix):
        count = matrix.shape[0]
        grouped = matrix.reshape(count, dp_count, seq_count, owner_rows)
        chosen = lax.dynamic_slice_in_dim(grouped, seq_place, 1, 2)
        return chosen.reshape(count, dp_count * owner_rows)

    normed_piece = lax.all_gather(normed, "seq", axis=0, tiled=True)
    proj_piece = lax.all_gather(grad_proj, "seq", axis=0, tiled=True)
    upstream_piece = lax.all_gather(upstream, "seq", axis=0, tiled=True)
    out_piece = lax.all_gather(normed_out, "seq", axis=0, tiled=True)
    first = lax.dot_general(
        select_rows(normed_piece),
        proj_piece,
        (((0,), (0,)), ((), ())),
        preferred_element_type=jnp.float32,
    )
    second = lax.dot_general(
        select_rows(upstream_piece),
        out_piece,
        (((0,), (0,)), ((), ())),
        preferred_element_type=jnp.float32,
    )
    in_part, out_part = (
        lax.psum_scatter(
            first.reshape(dp_count, owner_rows, grad_proj.shape[1]).astype(jnp.bfloat16),
            "dp",
            scatter_dimension=0,
            tiled=True,
        ).astype(jnp.float32),
        lax.psum_scatter(
            second.reshape(dp_count, owner_rows, normed_out.shape[1]).astype(jnp.bfloat16),
            "dp",
            scatter_dimension=0,
            tiled=True,
        ).astype(jnp.float32),
    )
    in_grad = in_part.reshape(owner_rows, grad_proj.shape[1])
    out_grad = out_part.reshape(owner_rows, normed_out.shape[1])
    vec_grad = lax.psum(vector, ("dp", "seq"))
    in_new, in_m_new, in_v_new = adamw_update(in_weight, in_grad, in_m, in_v)
    out_new, out_m_new, out_v_new = adamw_update(out_weight, out_grad, out_m, out_v)
    vec_new, vec_m_new, vec_v_new = adamw_update(vec_params, vec_grad, vec_m, vec_v)
    return (
        outputs[None],
        (upstream_f + grad_inputs)[None],
        in_grad,
        out_grad,
        vec_grad,
        in_new,
        out_new,
        vec_new,
        in_m_new,
        in_v_new,
        out_m_new,
        out_v_new,
        vec_m_new,
        vec_v_new,
    )


def solution(mesh):
    in_specs = (
        P("dp", "seq", None),
        P("dp", "seq", None),
        P("dp", None),
        P(("dp", "seq"), None),
        P(("dp", "seq"), None),
        P(("dp", "seq"), None),
        P(("dp", "seq"), None),
        P(("dp", "seq"), None),
        P(("dp", "seq"), None),
        P(),
        P(),
        P(),
    )
    out_specs = (
        P("dp", "seq", None),
        P("dp", "seq", None),
        P(("dp", "seq"), None),
        P(("dp", "seq"), None),
        P(),
        P(("dp", "seq"), None),
        P(("dp", "seq"), None),
        P(),
        P(("dp", "seq"), None),
        P(("dp", "seq"), None),
        P(("dp", "seq"), None),
        P(("dp", "seq"), None),
        P(),
        P(),
    )
    return jax.shard_map(body, mesh=mesh, in_specs=in_specs, out_specs=out_specs, check_vma=False)
```

profile of v0, /device:TPU:0, one launch (start us, length us, event | category | flops | bytes accessed | tf_op | source)
XLA Modules:
  0.0 677.7 jit_solution(5091734478298455227)
XLA Ops:
  15.3 2.6 compare_convert_fusion
  17.9 76.6 %all-gather.7.cloned.1.call-done = bf16[1024,4384]{1,0:T(8,128)(2,1)} async-done(((bf16[32,4384]{1,0:T(8,128)(2,1)}), bf16[1024,4384]{1,0:T(8,128)(2,1)}) %all-gather.7.cloned.1.call-update) | async-done | bytes 8978448 | tf_op jit(solution)/shard_map/all_gather | solution.py:155
  94.5 5.1 fusion.124
  101.4 2.7 collective-permute-start.2
  115.6 2.6 copy.208
  125.2 2.7 convolution_add_fusion
  128.1 150.3 %while.7 = (s32[]{:T(128)}, f32[32,64,128]{2,1,0:T(8,128)S(1)}, f32[1,32]{1,0:T(1,128)S(1)}, f32[32,64,128]{2,1,0:T(8,128)}, s32[]{:T(128)}) while((s32[]{:T(128)}, f32[32,64,128]{2,1,0:T(8,128)S(1)}, f32[1,32]{1,0:T(1,128)S(1)}, f32[32,64,128]{2,1,0:T(8,128)}, s32[]{:T(128)}) %tuple.149), condition=%wide.region_3.4_spmd, body=%wide.region_2.3_spmd.sunk | while | flops 524290 | bytes 7340261 | solution.py:198
  130.6 2.6 collective-permute-start
  138.1 22.7 %collective-permute-start = (f32[32,64,128]{2,1,0:T(8,128)}, f32[32,64,128]{2,1,0:T(8,128)S(1)}, u32[]{:S(2)}, u32[]{:S(2)}) collective-permute-start(f32[32,64,128]{2,1,0:T(8,128)} %multiply_add_fusion.13), channel_id=1, source_target_pairs={{0,1},{1,2},{2,3},{3,4},{4,5},{5,6},{6,7},{8,9},{9,10},{10,11},{11... | collective-permute-start | bytes 3145736 | tf_op jit(solution)/shard_map/while/body/eval_jaxpr/ppermute | solution.py:29
  165.6 26.2 %collective-permute-start = (f32[32,64,128]{2,1,0:T(8,128)}, f32[32,64,128]{2,1,0:T(8,128)S(1)}, u32[]{:S(2)}, u32[]{:S(2)}) collective-permute-start(f32[32,64,128]{2,1,0:T(8,128)} %multiply_add_fusion.13), channel_id=1, source_target_pairs={{0,1},{1,2},{2,3},{3,4},{4,5},{5,6},{6,7},{8,9},{9,10},{10,11},{11... | collective-permute-start | bytes 3145736 | tf_op jit(solution)/shard_map/while/body/eval_jaxpr/ppermute | solution.py:29
  196.6 18.5 %collective-permute-start = (f32[32,64,128]{2,1,0:T(8,128)}, f32[32,64,128]{2,1,0:T(8,128)S(1)}, u32[]{:S(2)}, u32[]{:S(2)}) collective-permute-start(f32[32,64,128]{2,1,0:T(8,128)} %multiply_add_fusion.13), channel_id=1, source_target_pairs={{0,1},{1,2},{2,3},{3,4},{4,5},{5,6},{6,7},{8,9},{9,10},{10,11},{11... | collective-permute-start | bytes 3145736 | tf_op jit(solution)/shard_map/while/body/eval_jaxpr/ppermute | solution.py:29
  220.0 18.5 %collective-permute-start = (f32[32,64,128]{2,1,0:T(8,128)}, f32[32,64,128]{2,1,0:T(8,128)S(1)}, u32[]{:S(2)}, u32[]{:S(2)}) collective-permute-start(f32[32,64,128]{2,1,0:T(8,128)} %multiply_add_fusion.13), channel_id=1, source_target_pairs={{0,1},{1,2},{2,3},{3,4},{4,5},{5,6},{6,7},{8,9},{9,10},{10,11},{11... | collective-permute-start | bytes 3145736 | tf_op jit(solution)/shard_map/while/body/eval_jaxpr/ppermute | solution.py:29
  243.4 13.9 %collective-permute-start = (f32[32,64,128]{2,1,0:T(8,128)}, f32[32,64,128]{2,1,0:T(8,128)S(1)}, u32[]{:S(2)}, u32[]{:S(2)}) collective-permute-start(f32[32,64,128]{2,1,0:T(8,128)} %multiply_add_fusion.13), channel_id=1, source_target_pairs={{0,1},{1,2},{2,3},{3,4},{4,5},{5,6},{6,7},{8,9},{9,10},{10,11},{11... | collective-permute-start | bytes 3145736 | tf_op jit(solution)/shard_map/while/body/eval_jaxpr/ppermute | solution.py:29
  262.1 13.9 %collective-permute-start = (f32[32,64,128]{2,1,0:T(8,128)}, f32[32,64,128]{2,1,0:T(8,128)S(1)}, u32[]{:S(2)}, u32[]{:S(2)}) collective-permute-start(f32[32,64,128]{2,1,0:T(8,128)} %multiply_add_fusion.13), channel_id=1, source_target_pairs={{0,1},{1,2},{2,3},{3,4},{4,5},{5,6},{6,7},{8,9},{9,10},{10,11},{11... | collective-permute-start | bytes 3145736 | tf_op jit(solution)/shard_map/while/body/eval_jaxpr/ppermute | solution.py:29
  278.4 2.7 broadcast_multiply_fusion.1
  281.1 2.6 copy.205
  286.1 3.5 fusion.25
  292.1 3.4 multiply_reduce_fusion.13
  295.6 4.3 multiply_reduce_fusion.7
  300.0 4.2 multiply_reduce_fusion.6
  304.2 2.6 copy.207
  306.7 5.2 fusion.35
  314.8 2.9 multiply_reduce_fusion.8
  318.4 2.8 fusion.54
  321.3 135.9 %while.16 = (s32[]{:T(128)}, f32[32,64,128]{2,1,0:T(8,128)S(1)}, f32[1,32]{1,0:T(1,128)S(1)}, f32[32,64,128]{2,1,0:T(8,128)}, s32[]{:T(128)}, /*index=5*/s32[]{:T(128)}) while((s32[]{:T(128)}, f32[32,64,128]{2,1,0:T(8,128)S(1)}, f32[1,32]{1,0:T(1,128)S(1)}, f32[32,64,128]{2,1,0:T(8,128)}, s32[]{:T(128)}, ...), condition=%wide.region_8.9_spmd.clone, body=%wide.region_7.8_spmd.clone.sunk | while | flops 1310723 | bytes 6291703 | solution.py:224
  324.9 14.3 %collective-permute-done.1 = bf16[32,64,128]{2,1,0:T(8,128)(2,1)} collective-permute-done((bf16[32,64,128]{2,1,0:T(8,128)(2,1)}, bf16[32,64,128]{2,1,0:T(8,128)(2,1)}, u32[]{:S(2)}, u32[]{:S(2)}) %collective-permute-start.1) | collective-permute-done | bytes 524320 | tf_op jit(solution)/shard_map/while/body/eval_jaxpr/ppermute | solution.py:29
  343.8 10.2 %collective-permute-done.1 = bf16[32,64,128]{2,1,0:T(8,128)(2,1)} collective-permute-done((bf16[32,64,128]{2,1,0:T(8,128)(2,1)}, bf16[32,64,128]{2,1,0:T(8,128)(2,1)}, u32[]{:S(2)}, u32[]{:S(2)}) %collective-permute-start.1) | collective-permute-done | bytes 524320 | tf_op jit(solution)/shard_map/while/body/eval_jaxpr/ppermute | solution.py:29
  358.6 40.5 %collective-permute-done.1 = bf16[32,64,128]{2,1,0:T(8,128)(2,1)} collective-permute-done((bf16[32,64,128]{2,1,0:T(8,128)(2,1)}, bf16[32,64,128]{2,1,0:T(8,128)(2,1)}, u32[]{:S(2)}, u32[]{:S(2)}) %collective-permute-start.1) | collective-permute-done | bytes 524320 | tf_op jit(solution)/shard_map/while/body/eval_jaxpr/ppermute | solution.py:29
  403.8 9.5 %collective-permute-done.1 = bf16[32,64,128]{2,1,0:T(8,128)(2,1)} collective-permute-done((bf16[32,64,128]{2,1,0:T(8,128)(2,1)}, bf16[32,64,128]{2,1,0:T(8,128)(2,1)}, u32[]{:S(2)}, u32[]{:S(2)}) %collective-permute-start.1) | collective-permute-done | bytes 524320 | tf_op jit(solution)/shard_map/while/body/eval_jaxpr/ppermute | solution.py:29
  418.0 9.5 %collective-permute-done.1 = bf16[32,64,128]{2,1,0:T(8,128)(2,1)} collective-permute-done((bf16[32,64,128]{2,1,0:T(8,128)(2,1)}, bf16[32,64,128]{2,1,0:T(8,128)(2,1)}, u32[]{:S(2)}, u32[]{:S(2)}) %collective-permute-start.1) | collective-permute-done | bytes 524320 | tf_op jit(solution)/shard_map/while/body/eval_jaxpr/ppermute | solution.py:29
  432.2 9.5 %collective-permute-done.1 = bf16[32,64,128]{2,1,0:T(8,128)(2,1)} collective-permute-done((bf16[32,64,128]{2,1,0:T(8,128)(2,1)}, bf16[32,64,128]{2,1,0:T(8,128)(2,1)}, u32[]{:S(2)}, u32[]{:S(2)}) %collective-permute-start.1) | collective-permute-done | bytes 524320 | tf_op jit(solution)/shard_map/while/body/eval_jaxpr/ppermute | solution.py:29
  446.3 9.5 %collective-permute-done.1 = bf16[32,64,128]{2,1,0:T(8,128)(2,1)} collective-permute-done((bf16[32,64,128]{2,1,0:T(8,128)(2,1)}, bf16[32,64,128]{2,1,0:T(8,128)(2,1)}, u32[]{:S(2)}, u32[]{:S(2)}) %collective-permute-start.1) | collective-permute-done | bytes 524320 | tf_op jit(solution)/shard_map/while/body/eval_jaxpr/ppermute | solution.py:29
  457.2 3.3 fusion.36
  465.9 2.6 reduce_window_sum.41
  468.5 2.6 reduce_window_sum.42
  475.6 5.1 fusion.28
  480.6 2.6 copy.212
  485.8 3.5 fusion.120
  491.8 3.1 convolution_bitcast_fusion.1
  505.2 7.9 %collective-permute-done.3 = f32[3,2304]{1,0:T(4,128)S(1)} collective-permute-done((f32[3,2304]{1,0:T(4,128)S(1)}, f32[3,2304]{1,0:T(4,128)S(1)}, u32[]{:S(2)}, u32[]{:S(2)}) %collective-permute-start.3) | collective-permute-done | bytes 27680 | tf_op jit(solution)/shard_map/ppermute | solution.py:29
  514.3 2.9 copy.218
  517.3 3.9 copy.220
  521.4 3.9 fusion.9
  525.6 4.7 fusion.31
  530.3 79.0 %all-gather.13.cloned.1.call-done = bf16[1024,4384]{1,0:T(8,128)(2,1)} async-done(((bf16[128,4384]{1,0:T(8,128)(2,1)}), bf16[1024,4384]{1,0:T(8,128)(2,1)}) %all-gather.13.cloned.1.call-update) | async-done | bytes 8978448 | tf_op jit(solution)/shard_map/all_gather | solution.py:271
  609.3 6.0 fusion.4
  616.7 6.9 %multiply_reduce_fusion.14 = (f32[1024]{0:T(1024)S(1)}, f32[128]{0:T(128)S(1)}, f32[128,1024]{1,0:T(8,128)S(1)}) fusion(f32[1,128,1024]{2,1,0:T(8,128)S(1)} %copy-done.2, f32[128]{0:T(128)S(1)} %copy-done.78, f32[1024]{0:T(1024)S(1)} %slice.169, bf16[128,4384]{1,0:T(8,128)(2,1)S(1)} %copy-done.3, bf16[1024,4384]{1,0:T(8,128)(2,1)} %all-gather.7.cloned.1.call-done), kind=kOutput, calls=%fused_computation.102 | convolution fusion | flops 1150024576 | bytes 11158528 | tf_op jit(solution)/shard_map/dot_general | solution.py:251
  623.7 39.2 %psum.7 = f32[14688]{0:T(1024)S(1)} all-reduce(f32[14688]{0:T(1024)S(1)} %concatenate.23), channel_id=1, replica_groups=mesh['dp'=4,'seq'=8] {'dp','seq'}, use_global_device_ids=true, to_apply=%region_33.34 | all-reduce | flops 14688 | bytes 117504 | tf_op jit(solution)/shard_map/psum | solution.py:302
  (309 shorter events, 138.3 us)
Async XLA Ops:
  7.2 87.3 %all-gather.7.cloned.1.call-start = ((), (), s32[]{:S(2)}) async-start(), calls=%async_computation.2 | async-start | bytes 9461760 | tf_op jit(solution)/shard_map/all_gather | solution.py:155
  9.1 286.4 %all-gather.9.cloned.1.call-start = ((), (), s32[]{:S(2)}) async-start(), calls=%async_computation.3 | async-start | bytes 4325376 | tf_op jit(solution)/shard_map/all_gather | solution.py:156
  9.9 504.4 %all-gather.11.cloned.1.call-start = ((), (), s32[]{:S(2)}) async-start(), calls=%async_computation.4 | async-start | bytes 2359296 | tf_op jit(solution)/shard_map/all_gather | solution.py:270
  10.1 5.2 copy-start.81
  10.1 5.0 copy-start.77
  11.0 506.3 %all-gather.15.cloned.1.call-start = ((), (), s32[]{:S(2)}) async-start(), calls=%async_computation.6 | async-start | bytes 2359296 | tf_op jit(solution)/shard_map/all_gather | solution.py:272
  11.8 509.5 %all-gather.17.cloned.1.call-start = ((), (), s32[]{:S(2)}) async-start(), calls=%async_computation.7 | async-start | bytes 4718592 | tf_op jit(solution)/shard_map/all_gather | solution.py:273
  13.3 90.8 %copy-start.76 = (f32[32]{0:T(128)}, f32[32]{0:T(128)S(1)}, u32[]{:S(2)}) copy-start(f32[32]{0:T(128)S(1)} %get-tuple-element.499) | copy-start | bytes 388
  13.3 91.0 %copy-start.59 = (f32[32]{0:T(128)}, f32[32]{0:T(128)S(1)}, u32[]{:S(2)}) copy-start(f32[32]{0:T(128)S(1)} %get-tuple-element.498) | copy-start | bytes 388
  17.9 101.3 %copy-start.65 = (f32[128]{0:T(128)}, f32[128]{0:T(128)S(1)}, u32[]{:S(2)}) copy-start(f32[128]{0:T(128)S(1)} %get-tuple-element.509) | copy-start | bytes 1540
  99.6 16.0 %copy-start.6 = (f32[128,4384]{1,0:T(8,128)}, f32[128,4384]{1,0:T(8,128)S(1)}, u32[]{:S(2)}) copy-start(f32[128,4384]{1,0:T(8,128)S(1)} %get-tuple-element.518) | copy-start | bytes 6733828
  101.4 16.9 %collective-permute-start.2 = (bf16[3,2304]{1,0:T(4,128)(2,1)}, bf16[3,2304]{1,0:T(4,128)(2,1)}, u32[]{:S(2)}, u32[]{:S(2)}) collective-permute-start(bf16[3,2304]{1,0:T(4,128)(2,1)} %slice.205), channel_id=1, source_target_pairs={{0,1},{1,2},{2,3},{3,4},{4,5},{5,6},{6,7},{8,9},{9,10},{10,11},{11... | collective-permute-start | bytes 41480 | tf_op jit(solution)/shard_map/ppermute | solution.py:29
  108.6 209.8 %copy-start.27 = (f32[128,32]{0,1:T(8,128)}, f32[128,32]{0,1:T(8,128)S(1)}, u32[]{:S(2)}) copy-start(f32[128,32]{0,1:T(8,128)S(1)} %copy.204) | copy-start | bytes 49156
  110.8 7.4 %copy-start.47 = (f32[128,32]{0,1:T(8,128)}, f32[128,32]{0,1:T(8,128)S(1)}, u32[]{:S(2)}) copy-start(f32[128,32]{0,1:T(8,128)S(1)} %copy.201) | copy-start | bytes 49156
  130.6 5.0 collective-permute-start
  138.1 25.1 %collective-permute-start = (f32[32,64,128]{2,1,0:T(8,128)}, f32[32,64,128]{2,1,0:T(8,128)S(1)}, u32[]{:S(2)}, u32[]{:S(2)}) collective-permute-start(f32[32,64,128]{2,1,0:T(8,128)} %multiply_add_fusion.13), channel_id=1, source_target_pairs={{0,1},{1,2},{2,3},{3,4},{4,5},{5,6},{6,7},{8,9},{9,10},{10,11},{11... | collective-permute-start | bytes 3145736 | tf_op jit(solution)/shard_map/while/body/eval_jaxpr/ppermute | solution.py:29
  165.6 28.6 %collective-permute-start = (f32[32,64,128]{2,1,0:T(8,128)}, f32[32,64,128]{2,1,0:T(8,128)S(1)}, u32[]{:S(2)}, u32[]{:S(2)}) collective-permute-start(f32[32,64,128]{2,1,0:T(8,128)} %multiply_add_fusion.13), channel_id=1, source_target_pairs={{0,1},{1,2},{2,3},{3,4},{4,5},{5,6},{6,7},{8,9},{9,10},{10,11},{11... | collective-permute-start | bytes 3145736 | tf_op jit(solution)/shard_map/while/body/eval_jaxpr/ppermute | solution.py:29
  196.6 21.0 %collective-permute-start = (f32[32,64,128]{2,1,0:T(8,128)}, f32[32,64,128]{2,1,0:T(8,128)S(1)}, u32[]{:S(2)}, u32[]{:S(2)}) collective-permute-start(f32[32,64,128]{2,1,0:T(8,128)} %multiply_add_fusion.13), channel_id=1, source_target_pairs={{0,1},{1,2},{2,3},{3,4},{4,5},{5,6},{6,7},{8,9},{9,10},{10,11},{11... | collective-permute-start | bytes 3145736 | tf_op jit(solution)/shard_map/while/body/eval_jaxpr/ppermute | solution.py:29
  220.0 21.0 %collective-permute-start = (f32[32,64,128]{2,1,0:T(8,128)}, f32[32,64,128]{2,1,0:T(8,128)S(1)}, u32[]{:S(2)}, u32[]{:S(2)}) collective-permute-start(f32[32,64,128]{2,1,0:T(8,128)} %multiply_add_fusion.13), channel_id=1, source_target_pairs={{0,1},{1,2},{2,3},{3,4},{4,5},{5,6},{6,7},{8,9},{9,10},{10,11},{11... | collective-permute-start | bytes 3145736 | tf_op jit(solution)/shard_map/while/body/eval_jaxpr/ppermute | solution.py:29
  243.4 16.3 %collective-permute-start = (f32[32,64,128]{2,1,0:T(8,128)}, f32[32,64,128]{2,1,0:T(8,128)S(1)}, u32[]{:S(2)}, u32[]{:S(2)}) collective-permute-start(f32[32,64,128]{2,1,0:T(8,128)} %multiply_add_fusion.13), channel_id=1, source_target_pairs={{0,1},{1,2},{2,3},{3,4},{4,5},{5,6},{6,7},{8,9},{9,10},{10,11},{11... | collective-permute-start | bytes 3145736 | tf_op jit(solution)/shard_map/while/body/eval_jaxpr/ppermute | solution.py:29
  262.1 16.3 %collective-permute-start = (f32[32,64,128]{2,1,0:T(8,128)}, f32[32,64,128]{2,1,0:T(8,128)S(1)}, u32[]{:S(2)}, u32[]{:S(2)}) collective-permute-start(f32[32,64,128]{2,1,0:T(8,128)} %multiply_add_fusion.13), channel_id=1, source_target_pairs={{0,1},{1,2},{2,3},{3,4},{4,5},{5,6},{6,7},{8,9},{9,10},{10,11},{11... | collective-permute-start | bytes 3145736 | tf_op jit(solution)/shard_map/while/body/eval_jaxpr/ppermute | solution.py:29
  281.1 4.9 copy-start.48
  281.1 4.9 copy-start.61
  284.6 4.9 copy-start.50
  295.6 4.4 copy-start.5
  295.6 4.4 copy-start.7
  295.6 4.4 copy-start.8
  321.3 288.0 %all-gather.13.cloned.1.call-start = ((), (), s32[]{:S(2)}) async-start(), calls=%async_computation.5 | async-start | bytes 10321920 | tf_op jit(solution)/shard_map/all_gather | solution.py:271
  323.6 15.6 %collective-permute-start.1 = (bf16[32,64,128]{2,1,0:T(8,128)(2,1)}, bf16[32,64,128]{2,1,0:T(8,128)(2,1)}, u32[]{:S(2)}, u32[]{:S(2)}) collective-permute-start(bf16[32,64,128]{2,1,0:T(8,128)(2,1)} %fusion.145), channel_id=1, source_target_pairs={{1,0},{2,1},{3,2},{4,3},{5,4},{6,5},{7,6},{9,8},{10,9},{11,10},{12... | collective-permute-start | bytes 1572872 | tf_op jit(solution)/shard_map/while/body/eval_jaxpr/ppermute | solution.py:29
  342.5 11.4 %collective-permute-start.1 = (bf16[32,64,128]{2,1,0:T(8,128)(2,1)}, bf16[32,64,128]{2,1,0:T(8,128)(2,1)}, u32[]{:S(2)}, u32[]{:S(2)}) collective-permute-start(bf16[32,64,128]{2,1,0:T(8,128)(2,1)} %fusion.145), channel_id=1, source_target_pairs={{1,0},{2,1},{3,2},{4,3},{5,4},{6,5},{7,6},{9,8},{10,9},{11,10},{12... | collective-permute-start | bytes 1572872 | tf_op jit(solution)/shard_map/while/body/eval_jaxpr/ppermute | solution.py:29
  357.4 41.8 %collective-permute-start.1 = (bf16[32,64,128]{2,1,0:T(8,128)(2,1)}, bf16[32,64,128]{2,1,0:T(8,128)(2,1)}, u32[]{:S(2)}, u32[]{:S(2)}) collective-permute-start(bf16[32,64,128]{2,1,0:T(8,128)(2,1)} %fusion.145), channel_id=1, source_target_pairs={{1,0},{2,1},{3,2},{4,3},{5,4},{6,5},{7,6},{9,8},{10,9},{11,10},{12... | collective-permute-start | bytes 1572872 | tf_op jit(solution)/shard_map/while/body/eval_jaxpr/ppermute | solution.py:29
  402.5 10.8 %collective-permute-start.1 = (bf16[32,64,128]{2,1,0:T(8,128)(2,1)}, bf16[32,64,128]{2,1,0:T(8,128)(2,1)}, u32[]{:S(2)}, u32[]{:S(2)}) collective-permute-start(bf16[32,64,128]{2,1,0:T(8,128)(2,1)} %fusion.145), channel_id=1, source_target_pairs={{1,0},{2,1},{3,2},{4,3},{5,4},{6,5},{7,6},{9,8},{10,9},{11,10},{12... | collective-permute-start | bytes 1572872 | tf_op jit(solution)/shard_map/while/body/eval_jaxpr/ppermute | solution.py:29
  416.7 10.8 %collective-permute-start.1 = (bf16[32,64,128]{2,1,0:T(8,128)(2,1)}, bf16[32,64,128]{2,1,0:T(8,128)(2,1)}, u32[]{:S(2)}, u32[]{:S(2)}) collective-permute-start(bf16[32,64,128]{2,1,0:T(8,128)(2,1)} %fusion.145), channel_id=1, source_target_pairs={{1,0},{2,1},{3,2},{4,3},{5,4},{6,5},{7,6},{9,8},{10,9},{11,10},{12... | collective-permute-start | bytes 1572872 | tf_op jit(solution)/shard_map/while/body/eval_jaxpr/ppermute | solution.py:29
  430.9 10.8 %collective-permute-start.1 = (bf16[32,64,128]{2,1,0:T(8,128)(2,1)}, bf16[32,64,128]{2,1,0:T(8,128)(2,1)}, u32[]{:S(2)}, u32[]{:S(2)}) collective-permute-start(bf16[32,64,128]{2,1,0:T(8,128)(2,1)} %fusion.145), channel_id=1, source_target_pairs={{1,0},{2,1},{3,2},{4,3},{5,4},{6,5},{7,6},{9,8},{10,9},{11,10},{12... | collective-permute-start | bytes 1572872 | tf_op jit(solution)/shard_map/while/body/eval_jaxpr/ppermute | solution.py:29
  445.0 10.8 %collective-permute-start.1 = (bf16[32,64,128]{2,1,0:T(8,128)(2,1)}, bf16[32,64,128]{2,1,0:T(8,128)(2,1)}, u32[]{:S(2)}, u32[]{:S(2)}) collective-permute-start(bf16[32,64,128]{2,1,0:T(8,128)(2,1)} %fusion.145), channel_id=1, source_target_pairs={{1,0},{2,1},{3,2},{4,3},{5,4},{6,5},{7,6},{9,8},{10,9},{11,10},{12... | collective-permute-start | bytes 1572872 | tf_op jit(solution)/shard_map/while/body/eval_jaxpr/ppermute | solution.py:29
  489.2 5.7 copy-start.28
  503.3 9.8 %collective-permute-start.3 = (f32[3,2304]{1,0:T(4,128)S(1)}, f32[3,2304]{1,0:T(4,128)S(1)}, u32[]{:S(2)}, u32[]{:S(2)}) collective-permute-start(f32[3,2304]{1,0:T(4,128)S(1)} %pad_add_fusion.1), channel_id=1, source_target_pairs={{1,0},{2,1},{3,2},{4,3},{5,4},{6,5},{7,6},{9,8},{10,9},{11,10},{12... | collective-permute-start | bytes 82952 | tf_op jit(solution)/shard_map/ppermute | solution.py:29
  505.1 8.0 %copy-start.19 = (bf16[128,2048]{1,0:T(8,128)(2,1)S(1)}, bf16[128,2048]{1,0:T(8,128)(2,1)}, u32[]{:S(2)}) copy-start(bf16[128,2048]{1,0:T(8,128)(2,1)} %get-tuple-element.479) | copy-start | bytes 1572868
  505.1 8.0 %copy-start.37 = (bf16[128,32]{1,0:T(8,128)(2,1)S(1)}, bf16[128,32]{1,0:T(8,128)(2,1)}, u32[]{:S(2)}) copy-start(bf16[128,32]{1,0:T(8,128)(2,1)} %get-tuple-element.473) | copy-start | bytes 24580
  514.3 151.4 %reduce-scatter.9.cloned.1.call-start = ((), (), s32[]{:S(2)}) async-start(), calls=%async_computation.9 | async-start | bytes 655360
  525.3 142.7 %reduce-scatter.7.cloned.1.call-start = ((), (), s32[]{:S(2)}) async-start(), calls=%async_computation.8 | async-start | bytes 1433600
  609.3 6.1 copy-start.83
  609.3 6.2 copy-start.78
  616.6 7.0 %copy-start.55 = (f32[2304]{0:T(1024)S(1)}, f32[2304]{0:T(1024)}, u32[]{:S(2)}) copy-start(f32[2304]{0:T(1024)} %get-tuple-element.436) | copy-start | bytes 27652
  616.6 7.0 %copy-start.58 = (f32[2048]{0:T(1024)S(1)}, f32[2048]{0:T(1024)}, u32[]{:S(2)}) copy-start(f32[2048]{0:T(1024)} %get-tuple-element.434) | copy-start | bytes 24580
  616.6 7.0 %copy-start.80 = (f32[32]{0:T(128)S(1)}, f32[32]{0:T(128)}, u32[]{:S(2)}) copy-start(f32[32]{0:T(128)} %get-tuple-element.472) | copy-start | bytes 388
  616.6 46.3 %copy-start.82 = (f32[128]{0:T(128)S(1)}, f32[128]{0:T(128)}, u32[]{:S(2)}) copy-start(f32[128]{0:T(128)} %copy-done.81) | copy-start | bytes 1540
  616.6 46.3 %copy-start.21 = (f32[1,128,1024]{2,1,0:T(8,128)S(1)}, f32[1,128,1024]{2,1,0:T(8,128)}, u32[]{:S(2)}) copy-start(f32[1,128,1024]{2,1,0:T(8,128)} %param.17) | copy-start | bytes 1572868
  (60 other events, 148.4 us)
Sparse Core Ops, SparseCore 0:
  11.4 82.9 all-gather.6
  98.1 60.3 all-gather.8
  160.6 31.1 all-gather.10
  193.9 31.2 all-gather.14
  321.4 75.3 all-gather.16
  514.4 94.9 all-gather.12
  612.7 23.5 reduce-scatter.8
  639.2 28.6 reduce-scatter.6
where the time goes:
time: 686 us; the launch traced here: 678 us
  waiting for transfers between devices  284 us (41%)
  starting transfers between devices  130 us (19%)
  other arithmetic  89.3 us (13%)
  matrix products  67.5 us (10%)
  local copies, waits for them, and re-layouts  51.8 us (8%)
  blocking collectives  39.2 us (6%)
  between operations  15.6 us (2%)
    ppermute x16, starting transfers between devices, shifted_2(): return lax.ppermute(block, axis, route)  129 us
    ppermute x16, waiting for transfers between devices, shifted_2(): return lax.ppermute(block, axis, route)  128 us
    all_gather x1, waiting for transfers between devices, body(): proj_piece = lax.all_gather(grad_proj, 'seq', axis=0, tiled=True)  79 us
    all_gather x1, waiting for transfers between devices, body(): lax.all_gather(in_weight.astype(jnp.bfloat16), ('dp', 'seq'), axis=0, til...  76.6 us
    psum x1, blocking collectives, body(): vec_grad = lax.psum(vector, ('dp', 'seq'))  39.2 us
    add x7, other arithmetic, relay(): return shifted_2(decay[:, None, None] * entry_now + local_state, 'seq', 1)  16.8 us
    convert_element_type x7, other arithmetic, back_relay(): (own_part + decay[:, None, None] * later).astype(jnp.bfloat16)  15.5 us
    dot_general x3, matrix products, ssd_block(): inside = jnp.einsum('hij,jhp->ihp', mixing, values, precision=top_precision)  13.7 us
  transfers between devices with their start and end apart: 24, of which 18 were waited for; matrix products, arithmetic and copies ran while one was open for 30% of the time, Pallas kernels for 0%

commit v1 on v0

v1 whole, which is shorter than its diff:
```python
import jax
import jax.numpy as jnp
from jax import lax
from jax.experimental import pallas as pl
from jax.experimental.pallas import tpu as pltpu
from jax.sharding import PartitionSpec as P

D = 1024
DI = 2048
H = 32
P_SIZE = 64
N = 128
KW = 4
STRETCH = 256
STEP = 10
CONV = 2304


norm_eps = 1e-05
beta_one = 0.9
beta_two = 0.95
learn_rate = 0.03
decay_rate = 0.1
adam_eps = 1e-08
top_precision = lax.Precision.HIGHEST


def unpack(vector):
    cursor = D + DI
    norm_gain = vector[:D]
    gate_gain = vector[D:cursor]
    conv_kernel = vector[cursor : cursor + KW * CONV].reshape(KW, CONV)
    cursor = cursor + KW * CONV
    conv_bias = vector[cursor : cursor + CONV]
    cursor = cursor + CONV
    step_bias = vector[cursor : cursor + H]
    log_rate = vector[cursor + H : cursor + 2 * H]
    skip_gain = vector[cursor + 2 * H : cursor + 3 * H]
    return (norm_gain, gate_gain, conv_kernel, conv_bias, step_bias, log_rate, skip_gain)


def repack(norm_gain, gate_gain, conv_kernel, conv_bias, step_bias, log_rate, skip_gain):
    return jnp.concatenate(
        [norm_gain, gate_gain, conv_kernel.reshape(-1), conv_bias, step_bias, log_rate, skip_gain]
    )


def input_norm(inputs, gain):
    scale = lax.rsqrt(jnp.mean(inputs * inputs, axis=-1, keepdims=True) + norm_eps)
    return inputs * scale * gain[None, :]


def gate_norm(ssd_out, gate_in, gain):
    mixed = ssd_out * jax.nn.silu(gate_in)
    scale = lax.rsqrt(jnp.mean(mixed * mixed, axis=-1, keepdims=True) + norm_eps)
    return mixed * scale * gain[None, :]


def conv_silu(padded, conv_kernel, conv_bias, ext_ids):
    length = padded.shape[0] - (KW - 1)
    own_ids = ext_ids[KW - 1 :]
    total = jnp.zeros((length, padded.shape[1]), jnp.float32) + conv_bias[None, :]
    for offset in range(KW):
        valid = (ext_ids[offset : offset + length] == own_ids).astype(jnp.float32)
        total = (
            total + conv_kernel[offset][None, :] * padded[offset : offset + length] * valid[:, None]
        )
    return jax.nn.silu(total)


def adamw_update(param, grad, first, second):
    first_new = beta_one * first + (1.0 - beta_one) * grad
    second_new = beta_two * second + (1.0 - beta_two) * grad * grad
    corrected = first_new / (1.0 - beta_one**STEP)
    scaled = jnp.sqrt(second_new / (1.0 - beta_two**STEP)) + adam_eps
    return (
        param * (1.0 - learn_rate * decay_rate) - learn_rate * corrected / scaled,
        first_new,
        second_new,
    )


CHUNK = 128
LANES = 128
bf16 = jnp.bfloat16
f32 = jnp.float32


def contract(a, b, left, right):
    return lax.dot_general(a, b, (((left,), (right,)), ((), ())), preferred_element_type=f32)


def spread_heads(table, heads, length):
    return jnp.concatenate(
        [jnp.broadcast_to(table[:, k : k + 1], (length, P_SIZE)) for k in range(heads)], axis=1
    )


def head_slice(block, k):
    return block[:, k * P_SIZE : (k + 1) * P_SIZE]


def chunk_terms(mixed_ref, raw_ref, meta_ref, ids_ref, small_ref, width):
    length = raw_ref.shape[0]
    values = mixed_ref[:, :width].astype(f32)
    input_map = mixed_ref[:, width : width + N]
    output_map = mixed_ref[:, width + N :]
    shifted_raw = raw_ref[...] + small_ref[0:1, :]
    step_size = jnp.maximum(shifted_raw, 0.0) + jnp.log1p(jnp.exp(-jnp.abs(shifted_raw)))
    rate = -jnp.exp(small_ref[1:2, :])
    log_decay = rate * step_size
    rows_index = lax.broadcasted_iota(jnp.int32, (length, length), 0)
    cols_index = lax.broadcasted_iota(jnp.int32, (length, length), 1)
    lower = rows_index >= cols_index
    cumulative = jnp.dot(
        lower.astype(f32), log_decay, precision=top_precision, preferred_element_type=f32
    )
    flipped = cumulative.T
    same = meta_ref[:, 0:1] == ids_ref[...]
    related = same & lower
    reach = meta_ref[:, 1:2] * jnp.exp(cumulative)
    tail = meta_ref[:, 2:3] * jnp.exp(cumulative[length - 1 :, :] - cumulative)
    scores = contract(output_map, input_map, 1, 1)

    def decay_of(k):
        spans = cumulative[:, k : k + 1] - flipped[k : k + 1, :]
        return jnp.exp(jnp.where(related, spans, -1e30))

    return (values, input_map, output_map, shifted_raw, step_size, rate, log_decay, same,
            rows_index, cols_index, reach, tail, scores, decay_of)


def forward_kernel(heads, mixed_ref, raw_ref, meta_ref, ids_ref, small_ref, out_ref, entry_ref, state):
    width = heads * P_SIZE
    length = raw_ref.shape[0]

    @pl.when(pl.program_id(0) == 0)
    def _():
        state[...] = jnp.zeros_like(state)

    (values, input_map, output_map, _, step_size, _, _, _, _, _, reach, tail, scores, decay_of) = (
        chunk_terms(mixed_ref, raw_ref, meta_ref, ids_ref, small_ref, width)
    )
    entry = state[...]
    entry_low = entry.astype(bf16)
    entry_ref[0] = entry_low
    fed = (values * spread_heads(step_size, heads, length)).astype(bf16)
    inside = []
    for k in range(heads):
        mixing = (scores * decay_of(k)).astype(bf16)
        inside.append(contract(mixing, head_slice(fed, k), 1, 0))
    wide_reach = spread_heads(reach, heads, length)
    out_ref[...] = jnp.concatenate(inside, axis=1) + wide_reach * contract(output_map, entry_low, 1, 0)
    weighted = (fed.astype(f32) * spread_heads(tail, heads, length)).astype(bf16)
    state[...] = entry * wide_reach[length - 1 :, :] + contract(input_map, weighted, 0, 0)


def backward_kernel(heads, mixed_ref, raw_ref, meta_ref, ids_ref, small_ref, skip_ref, ssd_ref,
                    entry_ref, grad_ref, gmix_ref, graw_ref, totals_ref, later, carry):
    width = heads * P_SIZE
    length = raw_ref.shape[0]

    @pl.when(pl.program_id(0) == 0)
    def _():
        later[...] = jnp.zeros_like(later)
        carry[...] = jnp.zeros_like(carry)
        totals_ref[...] = jnp.zeros_like(totals_ref)

    (values, input_map, output_map, shifted_raw, step_size, rate, log_decay, same, rows_index,
     cols_index, reach, tail, scores, decay_of) = chunk_terms(
        mixed_ref, raw_ref, meta_ref, ids_ref, small_ref, width
    )
    grad = grad_ref[...]
    grad_low = grad.astype(bf16)
    wide_step = spread_heads(step_size, heads, length)
    wide_reach = spread_heads(reach, heads, length)
    wide_tail = spread_heads(tail, heads, length)
    fed = (values * wide_step).astype(bf16)
    fed_full = fed.astype(f32)
    after = later[...]
    after_low = after.astype(bf16)
    grad_scores = jnp.zeros((length, length), f32)
    pieces = []
    for k in range(heads):
        decay = decay_of(k)
        mixing = (scores * decay).astype(bf16)
        own_grad = head_slice(grad_low, k)
        grad_scores = grad_scores + contract(own_grad, head_slice(fed, k), 1, 1) * decay
        pieces.append(contract(mixing, own_grad, 0, 0))
    grad_fed = jnp.concatenate(pieces, axis=1) + wide_tail * contract(input_map, after_low, 1, 0)
    reached = (grad * wide_reach).astype(bf16)
    weighted = (fed_full * wide_tail).astype(bf16)
    scores_low = grad_scores.astype(bf16)
    gmix_ref[:, :width] = wide_step * grad_fed + skip_ref[...] * grad
    gmix_ref[:, width : width + N] = contract(scores_low, output_map, 0, 0) + contract(
        weighted, after_low, 1, 1
    )
    gmix_ref[:, width + N :] = contract(scores_low, input_map, 1, 0) + contract(
        reached, entry_ref[0], 1, 1
    )
    later[...] = after * wide_reach[length - 1 :, :] + contract(output_map, reached, 0, 0)
    lane = lax.broadcasted_iota(jnp.int32, (length, LANES), 1)
    balance_wide = grad_low.astype(f32) * ssd_ref[...] - fed_full * grad_fed
    step_wide = values * grad_fed
    skip_wide = values * grad
    balance = jnp.zeros((length, LANES), f32)
    grad_step = jnp.zeros((length, LANES), f32)
    grad_skip = jnp.zeros((length, LANES), f32)
    for k in range(heads):
        here = lane == k
        balance = balance + jnp.where(here, jnp.sum(head_slice(balance_wide, k), axis=1, keepdims=True), 0.0)
        grad_step = grad_step + jnp.where(here, jnp.sum(head_slice(step_wide, k), axis=1, keepdims=True), 0.0)
        grad_skip = grad_skip + jnp.where(here, jnp.sum(head_slice(skip_wide, k), axis=1, keepdims=True), 0.0)
    following = (same & (rows_index <= cols_index)).astype(f32)
    grad_log = jnp.dot(
        following, balance, precision=top_precision, preferred_element_type=f32
    ) + meta_ref[:, 3:4] * carry[0:1, :]
    carry[0:1, :] = grad_log[0:1, :]
    grad_step = grad_step + rate * grad_log
    grad_raw = grad_step * jax.nn.sigmoid(shifted_raw)
    graw_ref[...] = grad_raw
    totals_ref[0:1, :] += jnp.sum(grad_raw, axis=0, keepdims=True)
    totals_ref[1:2, :] += jnp.sum(grad_log * log_decay, axis=0, keepdims=True)
    totals_ref[2:3, :] += jnp.sum(grad_skip, axis=0, keepdims=True)


def ssd_specs(heads, place):
    width = heads * P_SIZE
    return [
        pl.BlockSpec((CHUNK, width + 2 * N), lambda c: (place(c), 0)),
        pl.BlockSpec((CHUNK, LANES), lambda c: (place(c), 0)),
        pl.BlockSpec((CHUNK, 8), lambda c: (place(c), 0)),
        pl.BlockSpec((1, CHUNK), lambda c: (0, place(c))),
        pl.BlockSpec((8, LANES), lambda c: (0, 0)),
    ]


def ssd_forward(heads, mixed, raw, meta, ids_row, small):
    length = mixed.shape[0]
    width = heads * P_SIZE
    count = length // CHUNK
    return pl.pallas_call(
        lambda *refs: forward_kernel(heads, *refs),
        grid=(count,),
        in_specs=ssd_specs(heads, lambda c: c),
        out_specs=[
            pl.BlockSpec((CHUNK, width), lambda c: (c, 0)),
            pl.BlockSpec((1, N, width), lambda c: (c, 0, 0)),
        ],
        out_shape=[
            jax.ShapeDtypeStruct((length, width), f32),
            jax.ShapeDtypeStruct((count, N, width), bf16),
        ],
        scratch_shapes=[pltpu.VMEM((N, width), f32)],
        cost_estimate=pl.CostEstimate(flops=4 * length * N * width, bytes_accessed=4 * length * width, transcendentals=length * CHUNK * heads),
        name="ssd_forward",
    )(mixed, raw, meta, ids_row, small)


def ssd_backward(heads, mixed, raw, meta, ids_row, small, skip, ssd, entries, grad):
    length = mixed.shape[0]
    width = heads * P_SIZE
    count = length // CHUNK
    place = lambda c: count - 1 - c
    return pl.pallas_call(
        lambda *refs: backward_kernel(heads, *refs),
        grid=(count,),
        in_specs=ssd_specs(heads, place)
        + [
            pl.BlockSpec((1, width), lambda c: (0, 0)),
            pl.BlockSpec((CHUNK, width), lambda c: (place(c), 0)),
            pl.BlockSpec((1, N, width), lambda c: (place(c), 0, 0)),
            pl.BlockSpec((CHUNK, width), lambda c: (place(c), 0)),
        ],
        out_specs=[
            pl.BlockSpec((CHUNK, width + 2 * N), lambda c: (place(c), 0)),
            pl.BlockSpec((CHUNK, LANES), lambda c: (place(c), 0)),
            pl.BlockSpec((8, LANES), lambda c: (0, 0)),
        ],
        out_shape=[
            jax.ShapeDtypeStruct((length, width + 2 * N), f32),
            jax.ShapeDtypeStruct((length, LANES), f32),
            jax.ShapeDtypeStruct((8, LANES), f32),
        ],
        scratch_shapes=[pltpu.VMEM((N, width), f32), pltpu.VMEM((8, LANES), f32)],
        cost_estimate=pl.CostEstimate(flops=12 * length * N * width, bytes_accessed=12 * length * width, transcendentals=length * CHUNK * heads),
        name="ssd_backward",
    )(mixed, raw, meta, ids_row, small, skip, ssd, entries, grad)


def position_table(ids):
    chunked = ids.reshape(-1, CHUNK)
    none = jnp.full((1,), -1, jnp.int32)
    prior = jnp.concatenate([none, chunked[:-1, -1]])[:, None]
    following = jnp.concatenate([chunked[1:, 0], none])[:, None]
    last = chunked[:, -1:]
    columns = [chunked, chunked == prior, chunked == last, chunked == following]
    columns = [column.astype(f32).reshape(-1) for column in columns]
    return jnp.stack(columns + [jnp.zeros_like(columns[0])] * 4, axis=1)


def body(tokens, cotangent, doc_ids, in_weight, out_weight, in_m, in_v, out_m, out_v, vec_params, vec_m, vec_v):
    seq_count = lax.axis_size("seq")
    place = lax.axis_index("seq")
    heads = H // seq_count
    width = DI // seq_count
    mixed_width = width + 2 * N
    owner_rows = in_weight.shape[0]
    inputs = tokens[0]
    upstream_f = cotangent[0]
    local_len = inputs.shape[0]
    norm_gain, gate_gain, conv_kernel, conv_bias, step_bias, log_rate, skip_gain = unpack(vec_params)

    def by_place(matrix):
        return matrix.reshape(matrix.shape[0], seq_count, -1).transpose(1, 0, 2)

    in_low = in_weight.astype(bf16)
    out_low = out_weight.astype(bf16)
    shared = jnp.broadcast_to(in_low[None, :, 2 * DI : DI + CONV], (seq_count, owner_rows, 2 * N))
    steps = jnp.pad(by_place(in_low[:, DI + CONV :]), ((0, 0), (0, 0), (0, LANES - heads)))
    blocks = jnp.concatenate(
        [by_place(in_low[:, :DI]), by_place(in_low[:, DI : 2 * DI]), shared, steps, by_place(out_low)], axis=2
    )
    normed = input_norm(inputs, norm_gain).astype(bf16)
    upstream = upstream_f.astype(bf16)
    exchanged = lax.all_to_all(blocks, "seq", 0, 0)
    weights = lax.all_gather(exchanged.reshape(seq_count * owner_rows, -1), "dp", axis=0, tiled=True)
    normed_all = lax.all_gather(normed, "seq", axis=0, tiled=True)
    upstream_all = lax.all_gather(upstream, "seq", axis=0, tiled=True)
    in_width = width + mixed_width + LANES
    in_work = weights[:, :in_width]
    out_work = weights[:, in_width:]

    ids = doc_ids[0]
    ext_ids = jnp.concatenate([jnp.full((KW - 1,), -1, jnp.int32), ids])
    meta = position_table(ids)
    ids_row = ids.astype(f32)[None, :]

    def own(vector, size):
        return lax.dynamic_slice_in_dim(vector, place * size, size, vector.ndim - 1)

    own_gate_gain = own(gate_gain, width)
    own_kernel = jnp.concatenate([own(conv_kernel[:, :DI], width), conv_kernel[:, DI:]], axis=1)
    own_cbias = jnp.concatenate([own(conv_bias[:DI], width), conv_bias[DI:]])
    own_skip = own(skip_gain, heads)
    small = jnp.pad(jnp.stack([own(step_bias, heads), own(log_rate, heads)]), ((0, 6), (0, LANES - heads)))
    wide_skip = jnp.repeat(own_skip, P_SIZE)[None, :]

    projected = jnp.dot(normed_all, in_work, preferred_element_type=f32)
    gate_in = projected[:, :width]
    conv_in = projected[:, width : width + mixed_width].astype(bf16)
    step_raw = projected[:, width + mixed_width :]
    padded = jnp.concatenate([jnp.zeros((KW - 1, mixed_width), bf16), conv_in]).astype(f32)
    mixed = conv_silu(padded, own_kernel, own_cbias, ext_ids).astype(bf16)
    ssd, entries = ssd_forward(heads, mixed, step_raw, meta, ids_row, small)

    grad_gated = jnp.dot(upstream_all, out_work, preferred_element_type=f32)
    values = mixed[:, :width].astype(f32)
    ssd_out = ssd + wide_skip * values
    gate_sig = jax.nn.sigmoid(gate_in)
    gate_act = gate_in * gate_sig
    product = ssd_out * gate_act
    scaled_grad = grad_gated * own_gate_gain[None, :]
    stats = jnp.stack([jnp.sum(product * product, axis=1), jnp.sum(scaled_grad * product, axis=1)])
    stats = lax.psum(stats, "seq")
    raw_out = (product * own_gate_gain[None, :]).astype(bf16)
    out_part = contract(raw_out, out_work, 1, 1).astype(bf16)
    out_sum = lax.psum_scatter(out_part, "seq", scatter_dimension=0, tiled=True).astype(f32)
    scale = lax.rsqrt(stats[0] / DI + norm_eps)
    pull = scale * scale * scale * stats[1] / DI
    own_scale = lax.dynamic_slice_in_dim(scale, place * local_len, local_len)
    outputs = inputs + out_sum * own_scale[:, None]
    grad_product = scaled_grad * scale[:, None] - product * pull[:, None]
    grad_ssd = grad_product * gate_act
    grad_gate_in = grad_product * ssd_out * (gate_sig * (1.0 + gate_in * (1.0 - gate_sig)))
    grad_gate_gain = jnp.sum(grad_gated * product * scale[:, None], axis=0)
    normed_out = (raw_out.astype(f32) * scale[:, None]).astype(bf16)
    out_grad_part = contract(upstream_all, normed_out, 0, 0)

    grad_mixed, grad_raw, totals = ssd_backward(
        heads, mixed, step_raw, meta, ids_row, small, wide_skip, ssd, entries, grad_ssd
    )
    _, conv_back = jax.vjp(
        lambda block, kernel, constant: conv_silu(block, kernel, constant, ext_ids), padded, own_kernel, own_cbias
    )
    grad_padded, grad_kernel, grad_cbias = conv_back(grad_mixed)
    grad_proj = jnp.concatenate([grad_gate_in, grad_padded[KW - 1 :], grad_raw], axis=1).astype(bf16)
    grad_normed_part = contract(grad_proj, in_work, 1, 1).astype(bf16)
    in_grad_part = contract(normed_all, grad_proj, 0, 0)
    grad_normed = lax.psum_scatter(grad_normed_part, "seq", scatter_dimension=0, tiled=True).astype(f32)
    weight_part = jnp.concatenate([in_grad_part, out_grad_part], axis=1).astype(bf16)
    weight_sum = lax.psum_scatter(weight_part, "dp", scatter_dimension=0, tiled=True)
    returned = lax.all_to_all(weight_sum.reshape(seq_count, owner_rows, -1), "seq", 0, 0).astype(f32)

    def gathered(start, size):
        return returned[:, :, start : start + size].transpose(1, 0, 2).reshape(owner_rows, -1)

    in_grad = jnp.concatenate(
        [
            gathered(0, width),
            gathered(width, width),
            jnp.sum(returned[:, :, 2 * width : 2 * width + 2 * N], axis=0),
            gathered(width + mixed_width, heads),
        ],
        axis=1,
    )
    out_grad = gathered(in_width, width)

    grad_norm_gain = jnp.sum(in_work.astype(f32) * in_grad_part, axis=1) / norm_gain

    def placed(part, full, size):
        return lax.dynamic_update_slice_in_dim(
            jnp.zeros(part.shape[:-1] + (full,), f32), part, place * size, part.ndim - 1
        )

    vector = repack(
        grad_norm_gain,
        placed(grad_gate_gain, DI, width),
        jnp.concatenate([placed(grad_kernel[:, :width], DI, width), grad_kernel[:, width:]], axis=1),
        jnp.concatenate([placed(grad_cbias[:width], DI, width), grad_cbias[width:]]),
        placed(totals[0, :heads], H, heads),
        placed(totals[1, :heads], H, heads),
        placed(totals[2, :heads], H, heads),
    )
    vec_grad = lax.psum(vector, ("dp", "seq"))
    _, norm_back = jax.vjp(lambda block: input_norm(block, norm_gain), inputs)
    (grad_inputs,) = norm_back(grad_normed)
    in_new, in_m_new, in_v_new = adamw_update(in_weight, in_grad, in_m, in_v)
    out_new, out_m_new, out_v_new = adamw_update(out_weight, out_grad, out_m, out_v)
    vec_new, vec_m_new, vec_v_new = adamw_update(vec_params, vec_grad, vec_m, vec_v)
    return (
        outputs[None],
        (upstream_f + grad_inputs)[None],
        in_grad,
        out_grad,
        vec_grad,
        in_new,
        out_new,
        vec_new,
        in_m_new,
        in_v_new,
        out_m_new,
        out_v_new,
        vec_m_new,
        vec_v_new,
    )


def solution(mesh):
    in_specs = (
        P("dp", "seq", None),
        P("dp", "seq", None),
        P("dp", None),
        P(("dp", "seq"), None),
        P(("dp", "seq"), None),
        P(("dp", "seq"), None),
        P(("dp", "seq"), None),
        P(("dp", "seq"), None),
        P(("dp", "seq"), None),
        P(),
        P(),
        P(),
    )
    out_specs = (
        P("dp", "seq", None),
        P("dp", "seq", None),
        P(("dp", "seq"), None),
        P(("dp", "seq"), None),
        P(),
        P(("dp", "seq"), None),
        P(("dp", "seq"), None),
        P(),
        P(("dp", "seq"), None),
        P(("dp", "seq"), None),
        P(("dp", "seq"), None),
        P(("dp", "seq"), None),
        P(),
        P(),
    )
    return jax.shard_map(body, mesh=mesh, in_specs=in_specs, out_specs=out_specs, check_vma=False)
```

time: 686 us -> 313 us (0.46); the launches traced: 678 us -> 312 us
  waiting for transfers between devices: 284 us -> 110 us
  starting transfers between devices: 130 us -> 4.49 us
  other arithmetic: 89.3 us -> 28.6 us
  blocking collectives: 39.2 us -> 91.8 us
  matrix products: 67.5 us -> 20.3 us
  local copies, waits for them, and re-layouts: 51.8 us -> 16.7 us
  Pallas kernels: 0 us -> 25.3 us
    ppermute x16 -> x0, starting transfers between devices: 129 us -> none  [shifted_2(): return lax.ppermute(block, axis, route)]
    ppermute x16 -> x0, waiting for transfers between devices: 128 us -> none  [shifted_2(): return lax.ppermute(block, axis, route)]
    all_gather x6 -> x3, waiting for transfers between devices: 156 us -> 49.1 us  [the longest x1 35.7 us: body(): lax.all_gather(exchanged.reshape(seq_count * owner_rows, -1), 'dp', axis=...]
    reduce_scatter x0 -> x3, waiting for transfers between devices: none -> 61.2 us  [the longest x1 38.6 us: body(): lax.psum_scatter(out_part, 'seq', scatter_dimension=0, tiled=True)]
    dot_general x20 -> x6, matrix products: 67.5 us -> 20.3 us  [the longest x4 11.4 us: contract(): lax.dot_general(a, b, (((left,), (right,)), ((), ())), preferred_element_...]
    all_to_all x0 -> x1, blocking collectives: none -> 37.4 us  [body(): exchanged = lax.all_to_all(blocks, 'seq', 0, 0)]
    convert_element_type x22 -> x9, other arithmetic: 33.6 us -> 6.62 us  [the longest x1 2.93 us: body(): mixed = conv_silu(padded, own_kernel, own_cbias, ext_ids).astype(bf16)]
    pallas_call x0 -> x2, Pallas kernels: none -> 25.3 us  [the longest x1 16.7 us: ssd_backward(): pl.pallas_call(lambda *refs: backward_kernel(heads, *refs), grid=(count,)...]
  transfers between devices with their start and end apart: 24 -> 7, of which waited for: 18 -> 4; matrix products, arithmetic and copies ran while one was open for 30% -> 11% of each run, Pallas kernels for 0% -> 3%
where the time goes in v1:
time: 313 us; the launch traced here: 312 us
  waiting for transfers between devices  110 us (35%)
  blocking collectives  91.8 us (29%)
  other arithmetic  28.6 us (9%)
  Pallas kernels  25.3 us (8%)
  matrix products  20.3 us (6%)
  local copies, waits for them, and re-layouts  16.7 us (5%)
  between operations  14.7 us (5%)
  starting transfers between devices  4.49 us (1%)
    psum x1, blocking collectives, body(): vec_grad = lax.psum(vector, ('dp', 'seq'))  38.8 us
    reduce_scatter x1, waiting for transfers between devices, body(): lax.psum_scatter(out_part, 'seq', scatter_dimension=0, tiled=True)  38.6 us
    all_to_all x1, blocking collectives, body(): exchanged = lax.all_to_all(blocks, 'seq', 0, 0)  37.4 us
    all_gather x1, waiting for transfers between devices, body(): lax.all_gather(exchanged.reshape(seq_count * owner_rows, -1), 'dp', axis=...  35.7 us
    reduce_scatter x1, waiting for transfers between devices, body(): lax.psum_scatter(grad_normed_part, 'seq', scatter_dimension=0, tiled=True)  22.5 us
    pallas_call x1, Pallas kernels, ssd_backward(): pl.pallas_call(lambda *refs: backward_kernel(heads, *refs), grid=(count,)...  16.7 us
    psum x1, blocking collectives, body(): stats = lax.psum(stats, 'seq')  15.7 us
    all_gather x1, waiting for transfers between devices, body(): upstream_all = lax.all_gather(upstream, 'seq', axis=0, tiled=True)  13.4 us
  transfers between devices with their start and end apart: 7, of which 4 were waited for; matrix products, arithmetic and copies ran while one was open for 11% of the time, Pallas kernels for 3%

profile of v1, /device:TPU:0, one launch (start us, length us, event | category | flops | bytes accessed | tf_op | source)
XLA Modules:
  0.0 312.2 jit_solution(700559720496591490)
XLA Ops:
  7.2 1.2 fusion.13
  8.4 0.7 slice.173
  9.1 1.9 fusion.15
  11.1 1.6 copy.83
  13.8 37.4 %all_to_all.10 = bf16[8,32,1152]{2,1,0:T(8,128)(2,1)S(1)} all-to-all(bf16[8,32,1152]{2,1,0:T(8,128)(2,1)S(1)} %copy.88), channel_id=1, replica_groups=mesh['dp'=4,'seq'=8] {'seq'}, dimensions={0} | all-to-all | bytes 1179648 | tf_op jit(solution)/shard_map/all_to_all | solution.py:326
  51.1 1.1 copy.89
  52.3 0.7 bitcast_convert_fusion
  53.4 0.6 broadcast_in_dim_reshape.3.refs_5_
  54.8 0.6 fusion.50
  55.7 1.0 copy.93.refs_2_
  56.8 0.6 select_maximum_fusion.refs_4_
  57.5 35.7 %all-gather.6.cloned.1.call-done = bf16[1024,1152]{0,1:T(8,128)(2,1)} async-done(((bf16[256,1152]{0,1:T(8,128)(2,1)}), bf16[1024,1152]{0,1:T(8,128)(2,1)}) %all-gather.6.cloned.1.call-update) | async-done | bytes 2359312 | tf_op jit(solution)/shard_map/all_gather | solution.py:327
  93.2 4.5 %fusion.4 = f32[1024,896]{1,0:T(8,128)S(1)} fusion(bf16[1024,1024]{1,0:T(8,128)(2,1)} %all-gather.4.cloned.1.call-done, bf16[1024,1152]{0,1:T(8,128)(2,1)} %all-gather.6.cloned.1.call-done), kind=kOutput, calls=%fused_computation.24 | convolution fusion | flops 1879048192 | bytes 7602176 | tf_op jit(solution)/shard_map/dot_general | solution.py:349
  97.7 0.9 slice.235.refs_1_
  99.0 0.7 copy-done.7
  99.7 2.9 multiply_convert_fusion
  102.6 8.6 %ssd_forward.1 = (f32[1024,256]{1,0:T(8,128)}, bf16[8,128,256]{2,1,0:T(8,128)(2,1)}) custom-call(bf16[1024,512]{1,0:T(8,128)(2,1)} %get-tuple-element.43.refs_0_, f32[1024,128]{1,0:T(8,128)} %slice.235.refs_1_, f32[1024,8]{1,0:T(8,128)} %copy.93.refs_2_, f32[1,1024]{1,0:T(1,128)} %get-tuple-element.75.refs_3_, f32[8,128]{1,0:T(8,128)} %select_maximum_fusion.refs_4_), custom_call_target="tpu_custom_call" | custom-call | flops 134217728 | bytes 1048576 | tf_op jit(solution)/shard_map/ssd_forward/pallas_call | solution.py:242
  111.2 13.4 %all-gather.8.cloned.1.call-done = bf16[1024,1024]{1,0:T(8,128)(2,1)} async-done(((bf16[128,1024]{1,0:T(8,128)(2,1)}), bf16[1024,1024]{1,0:T(8,128)(2,1)}) %all-gather.8.cloned.1.call-update) | async-done | bytes 2097168 | tf_op jit(solution)/shard_map/all_gather | solution.py:329
  124.5 4.4 %multiply_reduce_fusion.7 = (f32[1024]{0:T(1024)S(1)}, f32[1024]{0:T(1024)S(1)}, f32[1024,256]{1,0:T(8,128)}, f32[1024,256]{1,0:T(8,128)}) fusion(f32[256]{0:T(256)S(1)} %dynamic_slice.28, f32[1024,896]{1,0:T(8,128)} %copy-done.7, f32[1024,256]{1,0:T(8,128)} %get-tuple-element.19.refs_6_, bf16[1024,512]{1,0:T(8,128)(2,1)S(1)} %copy-done, f32[256]{0:T(256)S(1)} %mul.496, ...), kind=kOutput, calls=%fused_computation.35 | convolution fusion | flops 540276736 | bytes 7350272 | tf_op jit(solution)/shard_map/dot_general | solution.py:357
  129.0 15.7 %psum.14 = f32[2,1024]{1,0:T(2,128)S(1)} all-reduce(f32[2,1024]{1,0:T(2,128)S(1)} %pad_maximum_fusion.6), channel_id=1, replica_groups=mesh['dp'=4,'seq'=8] {'seq'}, use_global_device_ids=true, to_apply=%region_4.5 | all-reduce | flops 2048 | bytes 16384 | tf_op jit(solution)/shard_map/psum | solution.py:365
  144.7 4.1 %multiply_convert_fusion.2 = (bf16[1024,256]{1,0:T(8,128)(2,1)}, f32[1024,256]{1,0:T(8,128)}, f32[256]{0:T(256)S(1)}) fusion(f32[1024,896]{1,0:T(8,128)} %copy-done.7, f32[1024,256]{1,0:T(8,128)} %get-tuple-element.19.refs_6_, f32[1024,256]{1,0:T(8,128)} %get-tuple-element.42, f32[1024]{0:T(1024)S(1)} %fusion.25, f32[1024]{0:T(1024)S(1)} %bitcast.115, ...), kind=kLoop, calls=%fused_computation.32 | loop fusion | flops 5766912 | bytes 6302720 | tf_op jit(solution)/shard_map/convert.3
  148.8 16.7 %ssd_backward.1 = (f32[1024,512]{1,0:T(8,128)}, f32[1024,128]{1,0:T(8,128)}, f32[8,128]{1,0:T(8,128)}) custom-call(bf16[1024,512]{1,0:T(8,128)(2,1)} %get-tuple-element.43.refs_0_, f32[1024,128]{1,0:T(8,128)} %slice.235.refs_1_, f32[1024,8]{1,0:T(8,128)} %copy.93.refs_2_, f32[1,1024]{1,0:T(1,128)} %get-tuple-element.75.refs_3_, ...), custom_call_target="tpu_custom_call" | custom-call | flops 402653184 | bytes 3145728 | tf_op jit(solution)/shard_map/ssd_backward/pallas_call | solution.py:265
  165.5 1.1 convert.23
  166.6 3.7 %multiply_reduce_fusion.4 = (f32[512]{0:T(512)S(1)}, f32[512]{0:T(512)S(1)}, f32[512]{0:T(512)S(1)}, f32[512]{0:T(512)S(1)}, f32[512]{0:T(512)S(1)}, /*index=5*/f32[1024,512]{1,0:T(8,128)S(1)}) fusion(f32[1027,512]{1,0:T(8,128)S(1)} %pad_convert_fusion, f32[1024]{0:T(1024)S(1)} %get-tuple-element.84, f32[1024]{0:T(1024)S(1)} %get-tuple-element.83, ...), kind=kLoop, calls=%fused_computation.13 | loop fusion | flops 11007488 | bytes 14702592 | tf_op jit(solution)/shard_map/transpose(jvp())/reduce_sum | solution.py:66
  170.3 0.9 broadcast_multiply_fusion
  171.1 1.1 fusion.2
  172.3 0.7 copy-done.4
  173.0 0.8 fusion.6
  173.9 0.3 copy-done.12
  174.2 0.8 copy-done.17
  175.0 2.3 multiply_reduce_fusion
  177.3 1.6 pad_maximum_fusion
  179.0 5.2 %convolution_convert_fusion = bf16[1024,1024]{1,0:T(8,128)(2,1)} fusion(bf16[1024,1152]{0,1:T(8,128)(2,1)} %all-gather.6.cloned.1.call-done, bf16[1024,128]{1,0:T(8,128)(2,1)S(1)} %convert.23, bf16[1024,512]{1,0:T(8,128)(2,1)S(1)} %fusion.2, bf16[1024,256]{1,0:T(8,128)(2,1)S(1)} %copy-done.12), kind=kOutput, calls=%fused_computation.20 | convolution fusion | flops 1885601792 | bytes 5767168 | tf_op jit(solution)/shard_map/dot_general | solution.py:90
  184.2 3.1 convolution_convert_fusion.1
  188.1 0.8 bitcast_dynamic-update-slice_fusion.3
  188.9 0.8 bitcast_dynamic-update-slice_fusion.4
  189.7 0.8 bitcast_dynamic-update-slice_fusion.5
  190.5 38.8 %psum.15 = f32[14688]{0:T(1024)S(1)} all-reduce(f32[14688]{0:T(1024)S(1)} %concatenate.49), channel_id=1, replica_groups=mesh['dp'=4,'seq'=8] {'dp','seq'}, use_global_device_ids=true, to_apply=%region_16.17 | all-reduce | flops 14688 | bytes 117504 | tf_op jit(solution)/shard_map/psum | solution.py:425
  229.3 2.1 copy.96
  231.5 4.2 %all-to-all-start.1 = ((bf16[8,32,1152]{2,1,0:T(8,128)(2,1)}), bf16[8,32,1152]{2,1,0:T(8,128)(2,1)S(1)}, u32[]{:S(2)}, u32[]{:S(2)}) async-start(bf16[8,32,1152]{2,1,0:T(8,128)(2,1)} %bitcast.34), calls=%async_computation.4 | async-start | bytes 1179648 | tf_op jit(solution)/shard_map/all_to_all | solution.py:393
  235.7 0.7 divide_subtract_fusion.2
  236.4 22.5 %reduce-scatter.6.cloned.1.call-done = bf16[128,1024]{1,0:T(8,128)(2,1)} async-done(((bf16[1024,1024]{1,0:T(8,128)(2,1)}), bf16[128,1024]{1,0:T(8,128)(2,1)}) %reduce-scatter.6.cloned.1.call-update) | async-done | bytes 262160 | tf_op jit(solution)/shard_map/reduce_scatter | solution.py:390
  258.9 1.1 fusion.17
  260.1 38.6 %reduce-scatter.4.cloned.1.call-done = bf16[128,1024]{1,0:T(8,128)(2,1)} async-done(((bf16[1024,1024]{1,0:T(8,128)(2,1)}), bf16[128,1024]{1,0:T(8,128)(2,1)}) %reduce-scatter.4.cloned.1.call-update) | async-done | bytes 262160 | tf_op jit(solution)/shard_map/reduce_scatter | solution.py:368
  298.7 2.2 fusion.12
  301.5 0.5 copy-done.13
  301.9 1.9 divide_subtract_fusion.1
  303.9 1.5 divide_subtract_fusion
  (134 shorter events, 4.5 us)
Async XLA Ops:
  7.2 5.5 %copy-start.8 = (f32[32,2048]{1,0:T(8,128)S(1)}, f32[32,2048]{1,0:T(8,128)}, u32[]{:S(2)}) copy-start(f32[32,2048]{1,0:T(8,128)} %param.16) | copy-start | bytes 786436
  7.2 50.3 %all-gather.4.cloned.1.call-start = ((), (), s32[]{:S(2)}) async-start(), calls=%async_computation.5 | async-start | bytes 2359296 | tf_op jit(solution)/shard_map/all_gather | solution.py:328
  8.4 2.6 copy-start.20
  11.0 82.1 %all-gather.6.cloned.1.call-start = ((), (), s32[]{:S(2)}) async-start(), calls=%async_computation.6 | async-start | bytes 2949120 | tf_op jit(solution)/shard_map/all_gather | solution.py:327
  13.7 38.6 %copy-start.5 = (f32[1,128,1024]{2,1,0:T(8,128)S(1)}, f32[1,128,1024]{2,1,0:T(8,128)}, u32[]{:S(2)}) copy-start(f32[1,128,1024]{2,1,0:T(8,128)} %param.13) | copy-start | bytes 1572868
  13.7 39.4 %copy-start.14 = (f32[14688]{0:T(1024)S(1)}, f32[14688]{0:T(1024)}, u32[]{:S(2)}) copy-start(f32[14688]{0:T(1024)} %param.21) | copy-start | bytes 176260
  13.8 40.3 %slice-start.1 = ((f32[14688]{0:T(1024)}), f32[9216]{0:T(1024)S(1)}, s32[]{:S(2)}) async-start(f32[14688]{0:T(1024)} %param.21), calls=%async_computation.12 | async-start | bytes 73728 | tf_op jit(solution)/shard_map/slice | solution.py:32
  13.8 40.4 %copy-start.16 = (s32[1,1024]{1,0:T(1,128)S(1)}, s32[1,1024]{1,0:T(1,128)}, u32[]{:S(2)}) copy-start(s32[1,1024]{1,0:T(1,128)} %param.14) | copy-start | bytes 12292
  51.1 5.6 %slice-start = ((f32[14688]{0:T(1024)}), f32[256]{0:T(256)S(1)}, s32[]{:S(2)}) async-start(f32[14688]{0:T(1024)} %param.21), calls=%async_computation.11 | async-start | bytes 2048 | tf_op jit(solution)/shard_map/slice | solution.py:344
  52.2 72.3 %all-gather.8.cloned.1.call-start = ((), (), s32[]{:S(2)}) async-start(), calls=%async_computation.8 | async-start | bytes 2359296 | tf_op jit(solution)/shard_map/all_gather | solution.py:329
  53.0 176.3 %reduce-scatter.8.cloned.1.call-start = ((), (), s32[]{:S(2)}) async-start(), calls=%async_computation.10 | async-start | bytes 2949120 | tf_op jit(solution)/shard_map/reduce_scatter | solution.py:392
  97.7 2.0 copy-start.7
  102.6 21.9 %copy-start = (bf16[1024,512]{1,0:T(8,128)(2,1)S(1)}, bf16[1024,512]{1,0:T(8,128)(2,1)}, u32[]{:S(2)}) copy-start(bf16[1024,512]{1,0:T(8,128)(2,1)} %get-tuple-element.43.refs_0_) | copy-start | bytes 3145732
  171.1 1.2 copy-start.1
  171.1 1.9 copy-start.4
  171.1 2.8 copy-start.22
  173.0 1.2 copy-start.12
  173.0 2.0 copy-start.17
  178.9 80.0 %reduce-scatter.6.cloned.1.call-start = ((), (), s32[]{:S(2)}) async-start(), calls=%async_computation.9 | async-start | bytes 2359296 | tf_op jit(solution)/shard_map/reduce_scatter | solution.py:390
  184.2 114.5 %reduce-scatter.4.cloned.1.call-start = ((), (), s32[]{:S(2)}) async-start(), calls=%async_computation.7 | async-start | bytes 2359296 | tf_op jit(solution)/shard_map/reduce_scatter | solution.py:368
  187.4 48.4 %copy-start.18 = (f32[14688]{0:T(1024)S(1)}, f32[14688]{0:T(1024)}, u32[]{:S(2)}) copy-start(f32[14688]{0:T(1024)} %param.22) | copy-start | bytes 176260
  187.4 48.4 %copy-start.19 = (f32[14688]{0:T(1024)S(1)}, f32[14688]{0:T(1024)}, u32[]{:S(2)}) copy-start(f32[14688]{0:T(1024)} %param.23) | copy-start | bytes 176260
  187.4 71.5 %copy-start.2 = (f32[1,128,1024]{2,1,0:T(8,128)S(1)}, f32[1,128,1024]{2,1,0:T(8,128)}, u32[]{:S(2)}) copy-start(f32[1,128,1024]{2,1,0:T(8,128)} %param.12) | copy-start | bytes 1572868
  187.4 72.6 %copy-start.21 = (f32[128]{0:T(128)S(1)}, f32[128]{0:T(128)}, u32[]{:S(2)}) copy-start(f32[128]{0:T(128)} %copy-done.20) | copy-start | bytes 1540
  187.4 111.3 %copy-start.6 = (f32[1,128,1024]{2,1,0:T(8,128)S(1)}, f32[1,128,1024]{2,1,0:T(8,128)}, u32[]{:S(2)}) copy-start(f32[1,128,1024]{2,1,0:T(8,128)} %param.13) | copy-start | bytes 1572868
  229.3 71.6 %copy-start.15 = (f32[14688]{0:T(1024)}, f32[14688]{0:T(1024)S(1)}, u32[]{:S(2)}) copy-start(f32[14688]{0:T(1024)S(1)} %psum.15) | copy-start | bytes 176260
  231.5 69.4 %all-to-all-start.1 = ((bf16[8,32,1152]{2,1,0:T(8,128)(2,1)}), bf16[8,32,1152]{2,1,0:T(8,128)(2,1)S(1)}, u32[]{:S(2)}, u32[]{:S(2)}) async-start(bf16[8,32,1152]{2,1,0:T(8,128)(2,1)} %bitcast.34), calls=%async_computation.4 | async-start | bytes 1179648 | tf_op jit(solution)/shard_map/all_to_all | solution.py:393
  301.0 1.0 copy-start.13
  301.1 2.7 copy-start.3
  301.1 2.7 copy-start.10
  301.2 2.7 copy-start.11
  301.4 4.0 %copy-start.9 = (f32[8,4,8,256]{3,2,0,1:T(8,128)}, f32[8,4,8,256]{3,2,0,1:T(8,128)S(1)}, u32[]{:S(2)}) copy-start(f32[8,4,8,256]{3,2,0,1:T(8,128)S(1)} %copy.109) | copy-start | bytes 786436
Sparse Core Ops, SparseCore 0:
  11.1 43.9 all-gather.3
  57.0 36.1 all-gather.5
  95.3 29.1 all-gather.7
  179.1 36.0 reduce-scatter.7
  217.3 41.6 reduce-scatter.5
  261.1 37.5 reduce-scatter.3

commit v2 on v1

--- a/solution.py
+++ b/solution.py
@@ -299,6 +299,244 @@
     return jnp.stack(columns + [jnp.zeros_like(columns[0])] * 4, axis=1)
 
 
+MESH = pl.DeviceIdType.MESH
+in_vmem = pl.BlockSpec(memory_space=pltpu.VMEM)
+
+
+def beyond(axis, distance):
+    count = lax.axis_size(axis)
+    return lax.rem(lax.axis_index(axis) + distance + count, count)
+
+
+def greet(axes):
+    barrier = pltpu.get_barrier_semaphore()
+    total = 0
+    for axis in axes:
+        for step in range(1, lax.axis_size(axis)):
+            pl.semaphore_signal(barrier, inc=1, device_id={axis: beyond(axis, step)}, device_id_type=MESH)
+            total += 1
+    pl.semaphore_wait(barrier, total)
+
+
+def push(source, target, send_sem, recv_sem, axis, peer):
+    return pltpu.make_async_remote_copy(
+        src_ref=source, dst_ref=target, send_sem=send_sem, recv_sem=recv_sem,
+        device_id={axis: peer}, device_id_type=MESH,
+    )
+
+
+def spread_kernel(seq_count, dp_count, blocks, out, seq_send, seq_recv, dp_send, dp_recv):
+    here, row = lax.axis_index("seq"), lax.axis_index("dp")
+    greet(("seq", "dp"))
+
+    def seq_copy(step, peer, slot):
+        return push(blocks.at[peer], out.at[row, slot], seq_send.at[step], seq_recv.at[step], "seq", peer)
+
+    def dp_copy(step, hop, from_row):
+        piece = beyond("seq", -step)
+        return push(out.at[row, piece], out.at[from_row, piece], dp_send.at[step, hop], dp_recv.at[step, hop], "dp", beyond("dp", hop))
+
+    def launch(step, _):
+        seq_copy(step, beyond("seq", step), here).start()
+        return 0
+
+    lax.fori_loop(1, seq_count, launch, 0)
+    for hop in range(1, dp_count):
+        push(blocks.at[here], out.at[row, here], dp_send.at[0, hop], dp_recv.at[0, hop], "dp", beyond("dp", hop)).start()
+    out[row, here] = blocks[here]
+
+    def relay(step, _):
+        seq_copy(step, beyond("seq", step), beyond("seq", -step)).wait_recv()
+        for hop in range(1, dp_count):
+            dp_copy(step, hop, row).start()
+        return 0
+
+    lax.fori_loop(1, seq_count, relay, 0)
+
+    def finish(step, _):
+        for hop in range(1, dp_count):
+            copy = dp_copy(step, hop, beyond("dp", -hop))
+            copy.wait_recv()
+            copy.wait_send()
+
+        @pl.when(step > 0)
+        def _():
+            seq_copy(step, beyond("seq", step), here).wait_send()
+
+        return 0
+
+    lax.fori_loop(0, seq_count, finish, 0)
+
+
+def spread_weights(blocks):
+    seq_count, dp_count = lax.axis_size("seq"), lax.axis_size("dp")
+    sems = pltpu.SemaphoreType.DMA
+    return pl.pallas_call(
+        lambda *refs: spread_kernel(seq_count, dp_count, *refs),
+        out_shape=jax.ShapeDtypeStruct((dp_count,) + blocks.shape, blocks.dtype),
+        in_specs=[in_vmem],
+        out_specs=in_vmem,
+        scratch_shapes=[sems((seq_count,)), sems((seq_count,)), sems((seq_count, dp_count)), sems((seq_count, dp_count))],
+        compiler_params=pltpu.CompilerParams(collective_id=1, has_side_effects=True),
+        name="spread_weights",
+    )(blocks)
+
+
+def sum_kernel(seq_count, part, out, got, send, recv):
+    greet(("seq",))
+    copies = [
+        push(part, got.at[step], send.at[step], recv.at[step], "seq", beyond("seq", step))
+        for step in range(1, seq_count)
+    ]
+    for copy in copies:
+        copy.start()
+    got[0] = part[...]
+    for copy in copies:
+        copy.wait_recv()
+    here = lax.axis_index("seq")
+    total = got[here]
+    for source in range(1, seq_count):
+        total = total + got[lax.rem(here - source + seq_count, seq_count)]
+    out[...] = total
+    for copy in copies:
+        copy.wait_send()
+
+
+def sum_over_seq(part):
+    seq_count = lax.axis_size("seq")
+    sems = pltpu.SemaphoreType.DMA
+    return pl.pallas_call(
+        lambda *refs: sum_kernel(seq_count, *refs),
+        out_shape=jax.ShapeDtypeStruct(part.shape, part.dtype),
+        in_specs=[in_vmem],
+        out_specs=in_vmem,
+        scratch_shapes=[pltpu.VMEM((seq_count,) + part.shape, part.dtype), sems((seq_count,)), sems((seq_count,))],
+        compiler_params=pltpu.CompilerParams(collective_id=2, has_side_effects=True),
+        name="sum_over_seq",
+    )(part)
+
+
+def reduce_kernel(seq_count, dp_count, part, vec, returned, vec_out, got, total, vec_dp, vec_row, vec_seq,
+                  dp_send, dp_recv, seq_send, seq_recv, va_send, va_recv, vb_send, vb_recv,
+                  vc_send, vc_recv, vd_send, vd_recv):
+    here, row = lax.axis_index("seq"), lax.axis_index("dp")
+    greet(("seq", "dp"))
+    hops = range(1, dp_count)
+    steps = range(1, seq_count)
+
+    def dp_copy(step, hop):
+        piece = beyond("seq", step)
+        peer = beyond("dp", hop)
+        return push(part.at[peer, piece], got.at[hop, piece], dp_send.at[step, hop], dp_recv.at[step, hop], "dp", peer)
+
+    first = [push(vec.at[beyond("dp", hop)], vec_dp.at[hop], va_send.at[hop], va_recv.at[hop], "dp", beyond("dp", hop)) for hop in hops]
+    for copy in first:
+        copy.start()
+
+    def launch(step, _):
+        for hop in hops:
+            dp_copy(lax.rem(step, seq_count), hop).start()
+        return 0
+
+    lax.fori_loop(1, seq_count + 1, launch, 0)
+    for copy in first:
+        copy.wait_recv()
+    sums = vec[row]
+    for hop in hops:
+        sums = sums + vec_dp[hop]
+    vec_row[...] = sums
+    second = [push(vec_row.at[beyond("seq", step)], vec_seq.at[step], vb_send.at[step], vb_recv.at[step], "seq", beyond("seq", step)) for step in steps]
+    for copy in second:
+        copy.start()
+    for copy in second:
+        copy.wait_recv()
+    final = vec_row[here]
+    for step in steps:
+        final = final + vec_seq[step]
+    vec_out[row, here] = final
+
+    def third(step, slot):
+        return push(vec_out.at[row, here], vec_out.at[row, slot], vc_send.at[step], vc_recv.at[step], "seq", beyond("seq", step))
+
+    for step in steps:
+        third(step, here).start()
+
+    def seq_copy(step, slot):
+        piece = beyond("seq", step)
+        return push(total.at[piece], returned.at[slot], seq_send.at[step], seq_recv.at[step], "seq", piece)
+
+    def combined(step):
+        piece = beyond("seq", step)
+        for hop in hops:
+            dp_copy(step, hop).wait_recv()
+        value = part[row, piece].astype(f32)
+        for hop in hops:
+            value = value + got[hop, piece].astype(f32)
+        return value.astype(bf16)
+
+    def exchange(step, _):
+        total[beyond("seq", step)] = combined(step)
+        seq_copy(step, here).start()
+        return 0
+
+    lax.fori_loop(1, seq_count, exchange, 0)
+    returned[here] = combined(0)
+
+    for step in steps:
+        third(step, beyond("seq", -step)).wait_recv()
+
+    def fourth(hop, slot):
+        return push(vec_out.at[row], vec_out.at[slot], vd_send.at[hop], vd_recv.at[hop], "dp", beyond("dp", hop))
+
+    for hop in hops:
+        fourth(hop, row).start()
+
+    def finish(step, _):
+        seq_copy(step, beyond("seq", -step)).wait_recv()
+        seq_copy(step, here).wait_send()
+        return 0
+
+    lax.fori_loop(1, seq_count, finish, 0)
+
+    def drain(step, _):
+        for hop in hops:
+            dp_copy(step, hop).wait_send()
+        return 0
+
+    lax.fori_loop(0, seq_count, drain, 0)
+    for hop in hops:
+        fourth(hop, beyond("dp", -hop)).wait_recv()
+        fourth(hop, row).wait_send()
+    for copy in first + second:
+        copy.wait_send()
+    for step in steps:
+        third(step, here).wait_send()
+
+
+def reduce_weights(part, vec):
+    seq_count, dp_count = lax.axis_size("seq"), lax.axis_size("dp")
+    sems = pltpu.SemaphoreType.DMA
+    piece = part.shape[2:]
+    lump = vec.shape[2:]
+    pairs = [(seq_count, dp_count)] * 2 + [(seq_count,)] * 2 + [(dp_count,)] * 2 + [(seq_count,)] * 4 + [(dp_count,)] * 2
+    return pl.pallas_call(
+        lambda *refs: reduce_kernel(seq_count, dp_count, *refs),
+        out_shape=[jax.ShapeDtypeStruct((seq_count,) + piece, bf16), jax.ShapeDtypeStruct(vec.shape, f32)],
+        in_specs=[in_vmem] * 2,
+        out_specs=[in_vmem] * 2,
+        scratch_shapes=[
+            pltpu.VMEM((dp_count, seq_count) + piece, bf16),
+            pltpu.VMEM((seq_count,) + piece, bf16),
+            pltpu.VMEM((dp_count, seq_count) + lump, f32),
+            pltpu.VMEM((seq_count,) + lump, f32),
+            pltpu.VMEM((seq_count,) + lump, f32),
+        ]
+        + [sems(pair) for pair in pairs],
+        compiler_params=pltpu.CompilerParams(collective_id=3, has_side_effects=True),
+        name="reduce_weights",
+    )(part, vec)
+
+
 def body(tokens, cotangent, doc_ids, in_weight, out_weight, in_m, in_v, out_m, out_v, vec_params, vec_m, vec_v):
     seq_count = lax.axis_size("seq")
     place = lax.axis_index("seq")
@@ -323,8 +561,7 @@
     )
     normed = input_norm(inputs, norm_gain).astype(bf16)
     upstream = upstream_f.astype(bf16)
-    exchanged = lax.all_to_all(blocks, "seq", 0, 0)
-    weights = lax.all_gather(exchanged.reshape(seq_count * owner_rows, -1), "dp", axis=0, tiled=True)
+    weights = spread_weights(blocks).reshape(D, -1)
     normed_all = lax.all_gather(normed, "seq", axis=0, tiled=True)
     upstream_all = lax.all_gather(upstream, "seq", axis=0, tiled=True)
     in_width = width + mixed_width + LANES
@@ -362,7 +599,7 @@
     product = ssd_out * gate_act
     scaled_grad = grad_gated * own_gate_gain[None, :]
     stats = jnp.stack([jnp.sum(product * product, axis=1), jnp.sum(scaled_grad * product, axis=1)])
-    stats = lax.psum(stats, "seq")
+    stats = sum_over_seq(stats.reshape(-1, LANES)).reshape(2, -1)
     raw_out = (product * own_gate_gain[None, :]).astype(bf16)
     out_part = contract(raw_out, out_work, 1, 1).astype(bf16)
     out_sum = lax.psum_scatter(out_part, "seq", scatter_dimension=0, tiled=True).astype(f32)
@@ -389,8 +626,31 @@
     in_grad_part = contract(normed_all, grad_proj, 0, 0)
     grad_normed = lax.psum_scatter(grad_normed_part, "seq", scatter_dimension=0, tiled=True).astype(f32)
     weight_part = jnp.concatenate([in_grad_part, out_grad_part], axis=1).astype(bf16)
-    weight_sum = lax.psum_scatter(weight_part, "dp", scatter_dimension=0, tiled=True)
-    returned = lax.all_to_all(weight_sum.reshape(seq_count, owner_rows, -1), "seq", 0, 0).astype(f32)
+    grad_norm_gain = jnp.sum(in_work.astype(f32) * in_grad_part, axis=1) / norm_gain
+
+    def placed(part, full, size):
+        return lax.dynamic_update_slice_in_dim(
+            jnp.zeros(part.shape[:-1] + (full,), f32), part, place * size, part.ndim - 1
+        )
+
+    vector = repack(
+        grad_norm_gain,
+        placed(grad_gate_gain, DI, width),
+        jnp.concatenate([placed(grad_kernel[:, :width], DI, width), grad_kernel[:, width:]], axis=1),
+        jnp.concatenate([placed(grad_cbias[:width], DI, width), grad_cbias[width:]]),
+        placed(totals[0, :heads], H, heads),
+        placed(totals[1, :heads], H, heads),
+        placed(totals[2, :heads], H, heads),
+    )
+    dp_count = lax.axis_size("dp")
+    devices = dp_count * seq_count
+    lines = -(-vector.shape[0] // (devices * LANES))
+    packed = jnp.pad(vector, (0, devices * lines * LANES - vector.shape[0]))
+    returned, vec_sum = reduce_weights(
+        weight_part.reshape(dp_count, seq_count, owner_rows, -1), packed.reshape(dp_count, seq_count, lines, LANES)
+    )
+    returned = returned.astype(f32)
+    vec_grad = vec_sum.reshape(-1)[: vector.shape[0]]
 
     def gathered(start, size):
         return returned[:, :, start : start + size].transpose(1, 0, 2).reshape(owner_rows, -1)
@@ -406,23 +666,6 @@
     )
     out_grad = gathered(in_width, width)
 
-    grad_norm_gain = jnp.sum(in_work.astype(f32) * in_grad_part, axis=1) / norm_gain
-
-    def placed(part, full, size):
-        return lax.dynamic_update_slice_in_dim(
-            jnp.zeros(part.shape[:-1] + (full,), f32), part, place * size, part.ndim - 1
-        )
-
-    vector = repack(
-        grad_norm_gain,
-        placed(grad_gate_gain, DI, width),
-        jnp.concatenate([placed(grad_kernel[:, :width], DI, width), grad_kernel[:, width:]], axis=1),
-        jnp.concatenate([placed(grad_cbias[:width], DI, width), grad_cbias[width:]]),
-        placed(totals[0, :heads], H, heads),
-        placed(totals[1, :heads], H, heads),
-        placed(totals[2, :heads], H, heads),
-    )
-    vec_grad = lax.psum(vector, ("dp", "seq"))
     _, norm_back = jax.vjp(lambda block: input_norm(block, norm_gain), inputs)
     (grad_inputs,) = norm_back(grad_normed)
     in_new, in_m_new, in_v_new = adamw_update(in_weight, in_grad, in_m, in_v)

time: 313 us -> 218 us (0.70)
  blocking collectives: 91.8 us -> 0 us
  waiting for transfers between devices: 110 us -> 21.3 us
  Pallas kernels: 25.3 us -> 107 us
  other arithmetic: 28.6 us -> 32.8 us
  starting transfers between devices: 4.49 us -> 0.34 us
  matrix products: 20.3 us -> 23.6 us
    pallas_call x0 -> x3, Pallas kernels: none -> 81.7 us  [the longest x1 38.6 us: reduce_weights(): pl.pallas_call(lambda *refs: reduce_kernel(seq_count, dp_count, *refs), o...]
    psum x2 -> x0, blocking collectives: 54.4 us -> none  [the longest x1 38.8 us: body(): vec_grad = lax.psum(vector, ('dp', 'seq'))]
    all_to_all x1 -> x0, blocking collectives: 37.4 us -> none  [body(): exchanged = lax.all_to_all(blocks, 'seq', 0, 0)]
    all_gather x1 -> x0, waiting for transfers between devices: 35.7 us -> none  [body(): lax.all_gather(exchanged.reshape(seq_count * owner_rows, -1), 'dp', axis=...]
    reduce_scatter x1, waiting for transfers between devices: 38.6 us -> 8.58 us  [body(): lax.psum_scatter(out_part, 'seq', scatter_dimension=0, tiled=True)]
    reduce_scatter x1, waiting for transfers between devices: 22.5 us -> 0.01 us  [body(): lax.psum_scatter(grad_normed_part, 'seq', scatter_dimension=0, tiled=True)]
    all_to_all x1 -> x0, starting transfers between devices: 4.24 us -> none  [body(): lax.all_to_all(weight_sum.reshape(seq_count, owner_rows, -1), 'seq', 0, 0)]
    dot_general x4, matrix products: 11.4 us -> 14.8 us  [contract(): lax.dot_general(a, b, (((left,), (right,)), ((), ())), preferred_element_...]
  transfers between devices with their start and end apart: 7 -> 4, of which waited for: 4 -> 3; matrix products, arithmetic and copies ran while one was open for 11% -> 20% of each run, Pallas kernels for 3% -> 38%
where the time goes in v2:
time: 218 us; the launch traced here: 217 us
  Pallas kernels  107 us (49%)
  other arithmetic  32.8 us (15%)
  matrix products  23.6 us (11%)
  waiting for transfers between devices  21.3 us (10%)
  local copies, waits for them, and re-layouts  17.2 us (8%)
  between operations  14.3 us (7%)
    pallas_call x1, Pallas kernels, reduce_weights(): pl.pallas_call(lambda *refs: reduce_kernel(seq_count, dp_count, *refs), o...  38.6 us
    pallas_call x1, Pallas kernels, spread_weights(): pl.pallas_call(lambda *refs: spread_kernel(seq_count, dp_count, *refs), o...  36.3 us
    pallas_call x1, Pallas kernels, ssd_backward(): pl.pallas_call(lambda *refs: backward_kernel(heads, *refs), grid=(count,)...  16.7 us
    dot_general x4, matrix products, contract(): lax.dot_general(a, b, (((left,), (right,)), ((), ())), preferred_element_...  14.8 us
    all_gather x1, waiting for transfers between devices, body(): upstream_all = lax.all_gather(upstream, 'seq', axis=0, tiled=True)  12.3 us
    reduce_scatter x1, waiting for transfers between devices, body(): lax.psum_scatter(out_part, 'seq', scatter_dimension=0, tiled=True)  8.58 us
    pallas_call x1, Pallas kernels, ssd_forward(): pl.pallas_call(lambda *refs: forward_kernel(heads, *refs), grid=(count,),...  8.51 us
    pallas_call x1, Pallas kernels, sum_over_seq(): pl.pallas_call(lambda *refs: sum_kernel(seq_count, *refs), out_shape=jax....  6.92 us
  transfers between devices with their start and end apart: 4, of which 3 were waited for; matrix products, arithmetic and copies ran while one was open for 20% of the time, Pallas kernels for 38%

profile of v2, /device:TPU:0, one launch (start us, length us, event | category | flops | bytes accessed | tf_op | source)
XLA Modules:
  0.0 216.6 jit_solution(12022719872340245824)
XLA Ops:
  7.3 1.2 fusion.13
  8.5 0.7 slice.178
  9.2 1.9 fusion.15
  11.2 1.8 bitcast_convert_fusion
  13.3 0.6 broadcast_in_dim_reshape.3.refs_5_
  14.1 0.6 fusion.47
  16.1 1.0 copy.67.refs_2_
  18.0 0.8 copy-done.13
  18.8 36.3 %spread_weights.1 = bf16[4,8,32,1152]{3,2,1,0:T(8,128)(2,1)} custom-call(bf16[8,32,1152]{2,1,0:T(8,128)(2,1)} %copy-done.13), custom_call_target="tpu_custom_call" | custom-call | tf_op jit(solution)/shard_map/spread_weights/pallas_call | solution.py:374
  55.2 0.6 select_maximum_fusion.refs_4_
  56.3 4.5 %fusion.4 = f32[1024,896]{1,0:T(8,128)S(1)} fusion(bf16[1024,1024]{1,0:T(8,128)(2,1)} %all-gather.3.cloned.1.call-done, bf16[1024,1152]{1,0:T(8,128)(2,1)} %bitcast.111), kind=kOutput, calls=%fused_computation.24 | convolution fusion | flops 1879048192 | bytes 7602176 | tf_op jit(solution)/shard_map/dot_general | solution.py:586
  60.8 0.9 slice.241.refs_1_
  62.1 0.6 copy-done.8
  62.7 3.0 %multiply_convert_fusion = (bf16[1024,512]{1,0:T(8,128)(2,1)}, f32[1024,512]{1,0:T(8,128)}) fusion(f32[1027,512]{1,0:T(8,128)S(1)} %pad_convert_fusion, f32[512]{0:T(512)S(1)} %bitcast.137, f32[1024]{0:T(1024)S(1)} %get-tuple-element.87, f32[512]{0:T(512)S(1)} %bitcast.139, f32[1024]{0:T(1024)S(1)} %get-tuple-element.86, f32[512]{0:T(512)S(1)} %bitcast.135, ...), kind=kLoop, calls=%fused_computation.14 | loop fusion | flops 8388608 | bytes 11556864 | tf_op jit(solution)/shard_map/convert_element_type | solution.py:591
  65.7 8.5 %ssd_forward.1 = (f32[1024,256]{1,0:T(8,128)}, bf16[8,128,256]{2,1,0:T(8,128)(2,1)}) custom-call(bf16[1024,512]{1,0:T(8,128)(2,1)} %get-tuple-element.48.refs_0_, f32[1024,128]{1,0:T(8,128)} %slice.241.refs_1_, f32[1024,8]{1,0:T(8,128)} %copy.67.refs_2_, f32[1,1024]{1,0:T(1,128)} %get-tuple-element.78.refs_3_, f32[8,128]{1,0:T(8,128)} %select_maximum_fusion.refs_4_), custom_call_target="tpu_custom_call" | custom-call | flops 134217728 | bytes 1048576 | tf_op jit(solution)/shard_map/ssd_forward/pallas_call | solution.py:242
  74.2 12.3 %all-gather.5.cloned.1.call-done = bf16[1024,1024]{1,0:T(8,128)(2,1)} async-done(((bf16[128,1024]{1,0:T(8,128)(2,1)}), bf16[1024,1024]{1,0:T(8,128)(2,1)}) %all-gather.5.cloned.1.call-update) | async-done | bytes 2097168 | tf_op jit(solution)/shard_map/all_gather | solution.py:566
  86.5 4.3 %multiply_reduce_fusion.7 = (f32[1024]{0:T(1024)S(1)}, f32[1024]{0:T(1024)S(1)}, f32[1024,256]{1,0:T(8,128)}, f32[1024,256]{1,0:T(8,128)}) fusion(f32[256]{0:T(256)S(1)} %dynamic_slice.26, f32[1024,896]{1,0:T(8,128)} %copy-done.8, f32[1024,256]{1,0:T(8,128)} %get-tuple-element.21.refs_6_, bf16[1024,512]{1,0:T(8,128)(2,1)S(1)} %copy-done, f32[256]{0:T(256)S(1)} %mul.496, ...), kind=kOutput, calls=%fused_computation.35 | convolution fusion | flops 540276736 | bytes 7350272 | tf_op jit(solution)/shard_map/dot_general | solution.py:594
  90.8 0.6 reshape.239.refs_0_
  91.4 6.9 %sum_over_seq.1 = f32[16,128]{1,0:T(8,128)} custom-call(f32[16,128]{1,0:T(8,128)} %reshape.239.refs_0_), custom_call_target="tpu_custom_call" | custom-call | tf_op jit(solution)/shard_map/sum_over_seq/pallas_call | solution.py:408
  98.3 0.7 rsqrt_bitcast_fusion
  99.0 0.7 fusion.26
  99.7 4.1 %multiply_convert_fusion.2 = (bf16[1024,256]{1,0:T(8,128)(2,1)}, f32[1024,256]{1,0:T(8,128)}, f32[256]{0:T(256)S(1)}) fusion(f32[1024,896]{1,0:T(8,128)} %copy-done.8, f32[1024,256]{1,0:T(8,128)} %get-tuple-element.21.refs_6_, f32[1024,256]{1,0:T(8,128)} %get-tuple-element.47, f32[1024]{0:T(1024)S(1)} %fusion.26, f32[1024]{0:T(1024)S(1)} %rsqrt_bitcast_fusion, ...), kind=kLoop, calls=%fused_computation.32 | loop fusion | flops 5766912 | bytes 6302720 | tf_op jit(solution)/shard_map/convert.5
  103.8 16.7 %ssd_backward.1 = (f32[1024,512]{1,0:T(8,128)}, f32[1024,128]{1,0:T(8,128)}, f32[8,128]{1,0:T(8,128)}) custom-call(bf16[1024,512]{1,0:T(8,128)(2,1)} %get-tuple-element.48.refs_0_, f32[1024,128]{1,0:T(8,128)} %slice.241.refs_1_, f32[1024,8]{1,0:T(8,128)} %copy.67.refs_2_, f32[1,1024]{1,0:T(1,128)} %get-tuple-element.78.refs_3_, ...), custom_call_target="tpu_custom_call" | custom-call | flops 402653184 | bytes 3145728 | tf_op jit(solution)/shard_map/ssd_backward/pallas_call | solution.py:265
  120.5 1.1 convert.25
  121.6 3.8 %multiply_reduce_fusion.4 = (f32[512]{0:T(512)S(1)}, f32[512]{0:T(512)S(1)}, f32[512]{0:T(512)S(1)}, f32[512]{0:T(512)S(1)}, f32[512]{0:T(512)S(1)}, /*index=5*/f32[1024,512]{1,0:T(8,128)S(1)}) fusion(f32[1027,512]{1,0:T(8,128)S(1)} %pad_convert_fusion, f32[1024]{0:T(1024)S(1)} %get-tuple-element.87, f32[1024]{0:T(1024)S(1)} %get-tuple-element.86, ...), kind=kLoop, calls=%fused_computation.13 | loop fusion | flops 11007488 | bytes 14702592 | tf_op jit(solution)/shard_map/transpose(jvp())/reduce_sum | solution.py:66
  125.4 0.9 broadcast_multiply_fusion
  126.3 1.1 fusion.2
  127.4 1.0 copy-done.9
  128.4 3.7 %convolution_convert_fusion = bf16[1024,1024]{1,0:T(8,128)(2,1)} fusion(bf16[1024,1152]{1,0:T(8,128)(2,1)S(1)} %bitcast.113, bf16[1024,128]{1,0:T(8,128)(2,1)S(1)} %convert.25, bf16[1024,512]{1,0:T(8,128)(2,1)S(1)} %fusion.2, bf16[1024,256]{1,0:T(8,128)(2,1)S(1)} %copy-done.16), kind=kOutput, calls=%fused_computation.20 | convolution fusion | flops 1885601792 | bytes 5767168 | tf_op jit(solution)/shard_map/dot_general | solution.py:90
  132.4 0.6 dynamic_slice.27
  133.4 3.2 %fusion.6 = bf16[1024,256]{0,1:T(8,128)(2,1)} fusion(bf16[1024,1024]{1,0:T(8,128)(2,1)} %all-gather.5.cloned.1.call-done, f32[1024]{0:T(1024)S(1)} %rsqrt_bitcast_fusion, f32[1024,256]{1,0:T(8,128)S(1)} %copy-done.1, f32[256]{0:T(256)S(1)} %dynamic_slice.26), kind=kOutput, calls=%fused_computation.28 | convolution fusion | flops 538443776 | bytes 3675136 | tf_op jit(solution)/shard_map/dot_general | solution.py:90
  136.6 2.0 copy.70
  139.2 0.8 bitcast_dynamic-update-slice_fusion.2
  139.9 0.8 bitcast_dynamic-update-slice_fusion.3
  140.7 0.8 bitcast_dynamic-update-slice_fusion.4
  141.5 2.1 convolution_convert_fusion.1
  143.6 1.0 copy-done.17
  144.6 5.8 %multiply_reduce_fusion = (f32[1024]{0:T(1024)S(1)}, bf16[1024,896]{1,0:T(8,128)(2,1)}) fusion(bf16[1024,1152]{1,0:T(8,128)(2,1)S(1)} %bitcast.115, bf16[1024,1024]{1,0:T(8,128)(2,1)} %all-gather.3.cloned.1.call-done, bf16[1024,128]{1,0:T(8,128)(2,1)} %copy-done.20, bf16[1024,512]{1,0:T(8,128)(2,1)} %copy-done.9, bf16[1024,256]{1,0:T(8,128)(2,1)S(1)} %copy-done.17), kind=kOutput, calls=%fused_computation | convolution fusion | flops 1888222208 | bytes 7606272 | tf_op jit(solution)/shard_map/dot_general | solution.py:90
  150.5 0.6 pad.48
  151.1 3.2 %pad_maximum_fusion.refs_0_ = bf16[4,8,32,1152]{3,2,1,0:T(8,128)(2,1)} fusion(bf16[4,8,32,256]{3,2,1,0:T(8,128)(2,1)S(1)} %bitcast.116, bf16[4,8,32,896]{3,2,1,0:T(8,128)(2,1)} %bitcast.119), kind=kLoop, calls=%fused_computation.2 | loop fusion | flops 4718592 | bytes 4718592 | tf_op jit(solution)/shard_map/concatenate | solution.py:628
  154.3 38.6 %reduce_weights.1 = (bf16[8,32,1152]{2,1,0:T(8,128)(2,1)}, f32[4,8,4,128]{3,2,1,0:T(4,128)}) custom-call(bf16[4,8,32,1152]{3,2,1,0:T(8,128)(2,1)} %pad_maximum_fusion.refs_0_, f32[4,8,4,128]{3,2,1,0:T(4,128)} %bitcast.125), custom_call_target="tpu_custom_call" | custom-call | tf_op jit(solution)/shard_map/reduce_weights/pallas_call | solution.py:522
  192.9 1.2 convert_element_type.137
  194.9 0.7 divide_subtract_fusion.2
  195.6 1.0 divide_subtract_fusion.1
  196.7 1.5 divide_subtract_fusion
  198.2 1.1 fusion.17
  199.3 8.6 %reduce-scatter.3.cloned.1.call-done = bf16[128,1024]{1,0:T(8,128)(2,1)} async-done(((bf16[1024,1024]{1,0:T(8,128)(2,1)}), bf16[128,1024]{1,0:T(8,128)(2,1)}) %reduce-scatter.3.cloned.1.call-update) | async-done | bytes 262160 | tf_op jit(solution)/shard_map/reduce_scatter | solution.py:605
  207.9 2.2 %fusion.12 = (f32[1,128,1024]{2,1,0:T(8,128)}, f32[1,128,1024]{2,1,0:T(8,128)}) fusion(f32[1,128,1024]{2,1,0:T(8,128)S(1)} %copy-done.7, f32[1,128,1024]{2,1,0:T(8,128)S(1)} %copy-done.2, bf16[128,1024]{1,0:T(8,128)(2,1)} %reduce-scatter.5.cloned.1.call-done, f32[128]{0:T(128)S(1)} %multiply_multiply_fusion.7, f32[1024]{0:T(1024)S(1)} %slice.178, ...), kind=kLoop, calls=%fused_computation.50 | loop fusion | flops 1310720 | bytes 2627072 | tf_op jit(solution)/shard_map/broadcast_in_dim | solution.py:676
  (139 shorter events, 5.8 us)
Async XLA Ops:
  7.2 5.9 %copy-start.21 = (f32[14688]{0:T(1024)S(1)}, f32[14688]{0:T(1024)}, u32[]{:S(2)}) copy-start(f32[14688]{0:T(1024)} %param.21) | copy-start | bytes 176260
  7.2 7.5 %slice-start.1 = ((f32[14688]{0:T(1024)}), f32[9216]{0:T(1024)S(1)}, s32[]{:S(2)}) async-start(f32[14688]{0:T(1024)} %param.21), calls=%async_computation.7 | async-start | bytes 73728 | tf_op jit(solution)/shard_map/slice | solution.py:32
  7.2 6.8 %copy-start.23 = (s32[1,1024]{1,0:T(1,128)S(1)}, s32[1,1024]{1,0:T(1,128)}, u32[]{:S(2)}) copy-start(s32[1,1024]{1,0:T(1,128)} %param.14) | copy-start | bytes 12292
  7.2 7.6 %copy-start.4 = (f32[32,4384]{1,0:T(8,128)S(1)}, f32[32,4384]{1,0:T(8,128)}, u32[]{:S(2)}) copy-start(f32[32,4384]{1,0:T(8,128)} %param.15) | copy-start | bytes 1683460
  7.2 49.1 %all-gather.3.cloned.1.call-start = ((), (), s32[]{:S(2)}) async-start(), calls=%async_computation.2 | async-start | bytes 2359296 | tf_op jit(solution)/shard_map/all_gather | solution.py:565
  9.2 6.6 %copy-start.10 = (f32[32,2048]{1,0:T(8,128)S(1)}, f32[32,2048]{1,0:T(8,128)}, u32[]{:S(2)}) copy-start(f32[32,2048]{1,0:T(8,128)} %param.16) | copy-start | bytes 786436
  11.1 75.3 %all-gather.5.cloned.1.call-start = ((), (), s32[]{:S(2)}) async-start(), calls=%async_computation.4 | async-start | bytes 2359296 | tf_op jit(solution)/shard_map/all_gather | solution.py:566
  13.0 185.2 %reduce-scatter.5.cloned.1.call-start = ((), (), s32[]{:S(2)}) async-start(), calls=%async_computation.5 | async-start | bytes 2359296 | tf_op jit(solution)/shard_map/reduce_scatter | solution.py:627
  14.8 2.7 %copy-start.24 = (f32[4,2304]{1,0:T(4,128)}, f32[4,2304]{1,0:T(4,128)S(1)}, u32[]{:S(2)}) copy-start(f32[4,2304]{1,0:T(4,128)S(1)} %reshape.233) | copy-start | bytes 110596
  17.8 37.3 %slice-start = ((f32[14688]{0:T(1024)}), f32[256]{0:T(256)S(1)}, s32[]{:S(2)}) async-start(f32[14688]{0:T(1024)} %param.21), calls=%async_computation.6 | async-start | bytes 2048 | tf_op jit(solution)/shard_map/slice | solution.py:581
  17.9 37.3 %slice-start.3 = ((f32[4,2304]{1,0:T(4,128)}), f32[4,2048]{1,0:T(4,128)S(1)}, s32[]{:S(2)}) async-start(f32[4,2304]{1,0:T(4,128)} %copy-done.24), calls=%async_computation.9 | async-start | bytes 65536 | tf_op jit(solution)/shard_map/slice | solution.py:580
  17.9 38.0 %slice-start.2 = ((f32[4,2304]{1,0:T(4,128)}), f32[4,256]{1,0:T(4,128)S(1)}, s32[]{:S(2)}) async-start(f32[4,2304]{1,0:T(4,128)} %copy-done.24), calls=%async_computation.8 | async-start | bytes 8192 | tf_op jit(solution)/shard_map/slice | solution.py:580
  18.0 0.8 copy-start.13
  60.8 1.9 copy-start.8
  65.7 20.8 %copy-start = (bf16[1024,512]{1,0:T(8,128)(2,1)S(1)}, bf16[1024,512]{1,0:T(8,128)(2,1)}, u32[]{:S(2)}) copy-start(bf16[1024,512]{1,0:T(8,128)(2,1)} %get-tuple-element.48.refs_0_) | copy-start | bytes 3145732
  121.6 5.8 %copy-start.20 = (bf16[1024,128]{1,0:T(8,128)(2,1)}, bf16[1024,128]{1,0:T(8,128)(2,1)S(1)}, u32[]{:S(2)}) copy-start(bf16[1024,128]{1,0:T(8,128)(2,1)S(1)} %convert.25) | copy-start | bytes 786436
  126.3 2.1 copy-start.3
  126.3 2.1 copy-start.16
  127.4 1.0 copy-start.9
  132.1 1.2 copy-start.1
  132.2 75.7 %reduce-scatter.3.cloned.1.call-start = ((), (), s32[]{:S(2)}) async-start(), calls=%async_computation.3 | async-start | bytes 2359296 | tf_op jit(solution)/shard_map/reduce_scatter | solution.py:605
  143.6 1.0 copy-start.17
  144.6 5.8 %copy-start.22 = (f32[14688]{0:T(1024)S(1)}, f32[14688]{0:T(1024)}, u32[]{:S(2)}) copy-start(f32[14688]{0:T(1024)} %param.21) | copy-start | bytes 176260
  144.6 6.5 %copy-start.6 = (bf16[1024,256]{1,0:T(8,128)(2,1)S(1)}, bf16[1024,256]{1,0:T(8,128)(2,1)}, u32[]{:S(2)}) copy-start(bf16[1024,256]{1,0:T(8,128)(2,1)} %copy.70) | copy-start | bytes 1572868
  194.0 0.8 copy-start.25
  194.0 0.9 copy-start.26
  194.0 0.9 copy-start.27
  194.1 1.6 copy-start.11
  194.1 1.6 copy-start.18
  194.1 1.5 copy-start.19
  194.4 2.2 %copy-start.5 = (f32[32,4384]{1,0:T(8,128)S(1)}, f32[32,4384]{1,0:T(8,128)}, u32[]{:S(2)}) copy-start(f32[32,4384]{1,0:T(8,128)} %param.15) | copy-start | bytes 1683460
  194.4 2.2 %copy-start.14 = (f32[32,4384]{1,0:T(8,128)S(1)}, f32[32,4384]{1,0:T(8,128)}, u32[]{:S(2)}) copy-start(f32[32,4384]{1,0:T(8,128)} %param.17) | copy-start | bytes 1683460
  194.4 2.2 %copy-start.15 = (f32[32,4384]{1,0:T(8,128)S(1)}, f32[32,4384]{1,0:T(8,128)}, u32[]{:S(2)}) copy-start(f32[32,4384]{1,0:T(8,128)} %param.18) | copy-start | bytes 1683460
  194.5 3.7 %copy-start.12 = (f32[8,4,8,256]{3,2,0,1:T(8,128)}, f32[8,4,8,256]{3,2,0,1:T(8,128)S(1)}, u32[]{:S(2)}) copy-start(f32[8,4,8,256]{3,2,0,1:T(8,128)S(1)} %copy.87) | copy-start | bytes 786436
  196.6 1.5 copy-start.2
  196.6 11.2 %copy-start.7 = (f32[1,128,1024]{2,1,0:T(8,128)S(1)}, f32[1,128,1024]{2,1,0:T(8,128)}, u32[]{:S(2)}) copy-start(f32[1,128,1024]{2,1,0:T(8,128)} %param.13) | copy-start | bytes 1572868
  196.7 11.2 %copy-start.28 = (f32[128]{0:T(128)S(1)}, f32[128]{0:T(128)}, u32[]{:S(2)}) copy-start(f32[128]{0:T(128)} %dynamic_slice.27) | copy-start | bytes 1540
Sparse Core Ops, SparseCore 0:
  11.2 45.0 all-gather.2
  58.5 27.9 all-gather.4
  132.3 35.8 reduce-scatter.4
  170.3 37.4 reduce-scatter.2
